TPU v7x, 32 devices: a whole 2x2x4 slice. The times are simulated.
32 devices in a mesh: ctx: 8 (over z, y), ch: 4 (over x, core).
Axes of the slice: x: 2, y: 2, z: 4, core: 2. Of those that a mesh axis runs over, the one named last changes fastest.
Arguments:
- queries: bfloat16 [2048, 4096], P('ctx', 'ch'), may hold values from -6 to 6
- keys: bfloat16 [2048, 4096], P('ctx', 'ch'), may hold values from -6 to 6
- values: bfloat16 [2048, 4096], P('ctx', 'ch'), may hold values from -6 to 6
- long_filter: float32 [2048, 4096], P('ctx', 'ch'), may hold values from -1.05 to 1.05
- short_filters: float32 [3, 3, 4096], P(None, None, 'ch'), may hold values from -3.6 to 3.6
- skip: float32 [4096], P('ch'), may hold values from -1 to 1
- w_out: bfloat16 [4096, 8192], P('ch'), may hold values from -0.09375 to 0.09375
- d_out: bfloat16 [2048, 8192], P('ctx', 'ch'), may hold values from -6 to 6
Outputs:
- d_queries: bfloat16 [2048, 4096], P('ctx', 'ch')
- d_keys: bfloat16 [2048, 4096], P('ctx', 'ch')
- d_values: bfloat16 [2048, 4096], P('ctx', 'ch')
- d_long: float32 [2048, 4096], P('ctx', 'ch')
- d_short: float32 [3, 3, 4096], P(None, None, 'ch')
- d_skip: float32 [4096], P('ch')
All inputs are finite; a program needn't handle non-finite values.
Results may differ from a plain program's by a relative error of at most 0.0049.
Values may be sent and summed in bfloat16 or wider, within the bound.
A program may use at most 128 MiB of HBM per device.

v0:
```python
import functools
import math

import jax
import jax.numpy as jnp
import numpy as np
from jax import lax
from jax.experimental import pallas as pl
from jax.experimental.pallas import tpu as pltpu
from jax.sharding import PartitionSpec as P

PAD = 8
TAIL = 16
PARAMS = dict(vmem_limit_bytes=60 * 1024 * 1024)
F32 = jnp.float32
BF16 = jnp.bfloat16
MESH = pl.DeviceIdType.MESH


def split_table(table):
    table = table.astype(np.float32)
    high = table.astype(BF16)
    low = (table - high.astype(np.float32)).astype(BF16)
    return np.concatenate([high[None], low[None]], axis=0)


def tables(block):
    freq = np.arange(block)[:, None]
    place = np.arange(block)[None, :]
    angle = (2 * freq + 1) * place % (4 * block) * (math.pi / (2 * block))
    forward = np.concatenate([np.cos(angle), -np.sin(angle)], axis=0)
    return split_table(forward), split_table(forward.T / block)


def fill(scratch, before, own, after, rim):
    rows = own.shape[0]
    scratch[0:PAD, :] = jnp.zeros_like(scratch[0:PAD, :])
    scratch[PAD + rows :, :] = jnp.zeros_like(scratch[PAD + rows :, :])
    scratch[PAD - rim : PAD, :] = before.astype(F32)
    scratch[PAD : PAD + rows, :] = own.astype(F32)
    if after is not None:
        scratch[PAD + rows : PAD + rows + rim, :] = after.astype(F32)


def short(scratch, taps, rows, lanes, s):
    total = None
    for j in range(taps.shape[1]):
        term = taps[s, j : j + 1, lanes] * scratch[PAD - j : PAD - j + rows, :]
        total = term if total is None else total + term
    return total


def times(a, b):
    return a[0] * b[0] - a[1] * b[1], a[0] * b[1] + a[1] * b[0]


def conj_times(a, b):
    return a[0] * b[0] + a[1] * b[1], a[0] * b[1] - a[1] * b[0]


def add(a, b):
    return b if a is None else (a[0] + b[0], a[1] + b[1])


def spectra(table, blocks, spec):
    for at in range(0, len(blocks), 2):
        pair = blocks[at : at + 2]
        data = jnp.concatenate([ref[...] for ref, _, _ in pair], axis=1)
        out = jnp.dot(table[0], data, preferred_element_type=F32) + jnp.dot(
            table[1], data, preferred_element_type=F32
        )
        cw = data.shape[1] // len(pair)
        for p, (_, s, i) in enumerate(pair):
            spec[s, i] = out[:, p * cw : (p + 1) * cw]


def mix_spectra(first, spec, held):
    count, rows2, cw = spec.shape[1:]
    half = rows2 // 2
    step = 8
    sign = 1.0 - 2.0 * (lax.broadcasted_iota(jnp.int32, (step, cw), 0) % 2).astype(F32)
    zero = jnp.zeros((step, cw), F32)

    def primes(blocks):
        out = [blocks[0]]
        for d in range(1, count):
            re, im = blocks[d]
            old_re, old_im = blocks[d - 1]
            out.append((re - sign * old_im, im + sign * old_re))
        return out

    def chunk(r, carry):
        low = pl.ds(pl.multiple_of(r * step, step), step)
        high = pl.ds(pl.multiple_of(half + r * step, step), step)

        def load(s, i):
            return spec[s, i, low, :], spec[s, i, high, :]

        def save(s, i, value):
            spec[s, i, low, :] = value[0]
            spec[s, i, high, :] = value[1]

        def primed(s):
            values = primes([load(s, i) for i in range(count)])
            for i in range(count):
                save(s, i, values[i])
            return values

        if count <= 8 and first:
            taps = primed(1)
            mixed = [load(0, i) for i in range(count)]
            for i in range(count):
                total = None
                for d in range(i + 1):
                    total = add(total, times(taps[d], mixed[i - d]))
                save(2, i, total)
            return carry
        if count <= 8:
            grads = [load(2, i) for i in range(count)]
            for s in (1, 0):
                taps = [load(s, i) for i in range(count)]
                if s == 0:
                    taps = primes(taps)
                for b in range(count):
                    total = None
                    for e in range(count - b):
                        total = add(total, conj_times(taps[e], grads[b + e]))
                    save(s, b, total)
            return carry
        if first:
            primed(1)

            def one(b, inner):
                def of_y(d, total):
                    return add(total, times(load(1, d), load(0, b - d)))

                save(2, b, lax.fori_loop(0, b + 1, of_y, (zero, zero)))
                return inner

            lax.fori_loop(0, count, one, 0)
            return carry
        primed(0)

        def both(b, inner):
            def of_g(e, totals):
                grad = load(2, b + e)
                return (
                    add(totals[0], conj_times(load(1, e), grad)),
                    add(totals[1], conj_times(load(0, e), grad)),
                )

            pair = lax.fori_loop(0, count - b, of_g, ((zero, zero), (zero, zero)))
            for s in range(2):
                held[s, b, 0], held[s, b, 1] = pair[s]
            return inner

        lax.fori_loop(0, count, both, 0)
        for b in range(count):
            save(1, b, (held[0, b, 0], held[0, b, 1]))
            save(0, b, (held[1, b, 0], held[1, b, 1]))
        return carry

    lax.fori_loop(0, half // step, chunk, 0)


def back_pair(table, values):
    data = jnp.concatenate(values, axis=1)
    high = data.astype(BF16)
    low = (data - high.astype(F32)).astype(BF16)
    out = (
        jnp.dot(table[0], high, preferred_element_type=F32)
        + jnp.dot(table[0], low, preferred_element_type=F32)
        + jnp.dot(table[1], high, preferred_element_type=F32)
    )
    cw = data.shape[1] // len(values)
    return [out[:, p * cw : (p + 1) * cw].astype(BF16) for p in range(len(values))]


def greet(sizes):
    barrier = pltpu.get_barrier_semaphore()
    for axis, size in sizes:
        me = lax.axis_index(axis)
        for o in range(1, size):
            peer = lax.rem(me + o, size)
            pl.semaphore_signal(barrier, inc=1, device_id={axis: peer}, device_id_type=MESH)
    pl.semaphore_wait(barrier, sum(size - 1 for _, size in sizes))


def send(source, target, send_sem, recv_sem, peer, axis="ctx"):
    return pltpu.make_async_remote_copy(
        src_ref=source,
        dst_ref=target,
        send_sem=send_sem,
        recv_sem=recv_sem,
        device_id={axis: peer},
        device_id_type=MESH,
    )


def far_first(size):
    return sorted(range(1, size), key=lambda o: abs(o - size // 2))


def gather_kernel(q_ref, k_ref, v_ref, long_ref, taps, d_ref, w_hbm,
                  mh_ref, go_ref, before, after, ext, mh_tx, held, weights, total,
                  edge_sent, edge_came, sent, came, own_sent, pass_sent, d_came, w_sem):
    count, _, rows, cw = mh_ref.shape
    parts, halves = held.shape[:2]
    cols = d_ref.shape[1]
    piece = cols // halves
    rim = taps.shape[1] - 1
    me = lax.axis_index("ctx")
    mine = lax.axis_index("ch")
    partner = mine + 1 - 2 * lax.rem(mine, 2)
    greet([("ctx", count), ("ch", parts)])

    rest = [lax.rem(mine + 2 * o, parts) for o in range(1, parts // 2)]
    other = [lax.rem(partner + 2 * o, parts) for o in range(1, parts // 2)]
    after_me = lax.rem(me + 1, count)
    before_me = lax.rem(me + count - 1, count)

    edges = []
    for s, ref in ((1, k_ref), (2, v_ref), (0, q_ref)):
        edges.append(send(ref.at[rows - TAIL : rows], before.at[s], edge_sent.at[s],
                          edge_came.at[s], after_me))
    for s, ref in ((0, q_ref), (1, k_ref), (2, v_ref)):
        edges.append(send(ref.at[0:TAIL], after.at[s], edge_sent.at[3 + s],
                          edge_came.at[3 + s], before_me))
    for edge in edges:
        edge.start()

    def own(slot, half, peer):
        lanes = slice(half * piece, (half + 1) * piece)
        return send(d_ref.at[:, lanes], held.at[mine, half], own_sent.at[slot, half],
                    d_came.at[mine, half], peer, "ch")

    def passed(slot, half, part):
        return send(held.at[part, half], held.at[part, half], pass_sent.at[slot, half],
                    d_came.at[part, half], partner, "ch")

    for half in range(halves):
        for slot, peer in enumerate(rest + [partner]):
            own(slot, half, peer).start()

    def weight(part):
        lanes = pl.ds(pl.multiple_of(part * cols, cols), cols)
        return pltpu.make_async_copy(w_hbm.at[:, lanes], weights.at[part], w_sem.at[part])

    order = [mine, partner] + [p for pair in zip(rest, other) for p in pair]
    for part in order:
        weight(part).start()
    for edge in edges:
        edge.wait()

    @pl.when(me == 0)
    def _():
        before[...] = jnp.zeros_like(before)

    @pl.when(me == count - 1)
    def _():
        after[...] = jnp.zeros_like(after)

    for c in range(count):
        lanes = slice(c * cw, (c + 1) * cw)
        fill(ext, before[1, TAIL - rim :, lanes], k_ref[:, lanes], None, rim)
        keyed = short(ext, taps, rows, lanes, 1)
        fill(ext, before[2, TAIL - rim :, lanes], v_ref[:, lanes], None, rim)
        mh_tx[c, 0] = (keyed * short(ext, taps, rows, lanes, 2)).astype(BF16)
        mh_tx[c, 1] = long_ref[:, lanes].astype(BF16)

    def exchange(peer):
        return send(mh_tx.at[peer], mh_ref.at[me], sent.at[peer], came.at[me], peer)

    def arrival(peer):
        return send(mh_tx.at[peer], mh_ref.at[peer], sent.at[peer], came.at[peer], peer)

    peers = [lax.rem(me + o, count) for o in far_first(count)]
    for peer in peers:
        exchange(peer).start()
    mh_ref[me] = mh_tx[me]

    def product(data, part, half=None):
        lanes = slice(None) if half is None else slice(half * piece, (half + 1) * piece)
        return lax.dot_general(data, weights[part, :, lanes], (((1,), (1,)), ((), ())),
                               preferred_element_type=F32)

    def take(part, half):
        total[...] += product(held[part, half], part, half)

    weight(mine).wait()
    total[...] = product(d_ref[...], mine)
    weight(partner).wait()
    for half in range(halves):
        passed(0, half, partner).wait_recv()
        take(partner, half)
    for slot, (direct, relayed) in enumerate(zip(rest, other)):
        weight(direct).wait()
        weight(relayed).wait()
        for half in range(halves):
            passed(slot, half, direct).wait_recv()
            passed(slot, half, direct).start()
            take(direct, half)
            passed(slot, half, relayed).wait_recv()
            take(relayed, half)
    go_ref[...] = total[...].astype(BF16)

    for peer in peers:
        arrival(peer).wait_recv()
    for peer in peers:
        exchange(peer).wait_send()
    for half in range(halves):
        for slot, peer in enumerate(rest + [partner]):
            own(slot, half, peer).wait_send()
        for slot, direct in enumerate(rest):
            passed(slot, half, direct).wait_send()


def conv_kernel(q_ref, before, go_ref, taps, mh_ref, forward, inverse, y_ref, b_ref, edge_ref,
                ext, g_tx, g_rx, y_tx, b_tx, spec, held, sent, came, edge_sem):
    count, _, rows, cw = mh_ref.shape
    rim = taps.shape[1] - 1
    me = lax.axis_index("ctx")
    greet([("ctx", count)])
    edge_rows = edge_ref.shape[0]
    previous = lax.rem(me + count - 1, count)
    edge = send(go_ref.at[0:edge_rows], edge_ref, edge_sem.at[0], edge_sem.at[1], previous)
    edge.start()
    for c in range(count):
        lanes = slice(c * cw, (c + 1) * cw)
        fill(ext, before[0, TAIL - rim :, lanes], q_ref[:, lanes], None, rim)
        g_tx[c] = (go_ref[:, lanes].astype(F32) * short(ext, taps, rows, lanes, 0)).astype(BF16)

    def exchange(kind, source, target, peer):
        return send(
            source.at[peer], target.at[me], sent.at[kind, peer], came.at[kind, me], peer
        )

    def arrival(kind, source, target, peer):
        return send(
            source.at[peer], target.at[peer], sent.at[kind, peer], came.at[kind, peer], peer
        )

    peers = [lax.rem(me + o, count) for o in far_first(count)]
    for peer in peers:
        exchange(0, g_tx, g_rx, peer).start()
    g_rx[me] = g_tx[me]

    blocks = []
    for i in range(count):
        blocks += [(mh_ref.at[i, 0], 0, i), (mh_ref.at[i, 1], 1, i)]
    spectra(forward, blocks, spec)
    mix_spectra(True, spec, held)
    for i in range(0, count, 2):
        for p, value in enumerate(back_pair(inverse, [spec[2, i], spec[2, i + 1]])):
            y_tx[i + p, 0:rows, :] = value
            if i + p > 0:
                y_tx[i + p - 1, rows : rows + TAIL, :] = value[:TAIL]
    y_tx[count - 1, rows : rows + TAIL, :] = jnp.zeros((TAIL, cw), BF16)
    for peer in peers:
        exchange(1, y_tx, y_ref, peer).start()
    y_ref[me] = y_tx[me]

    for peer in peers:
        arrival(0, g_tx, g_rx, peer).wait_recv()
    spectra(forward, [(g_rx.at[i], 2, i) for i in range(count)], spec)
    mix_spectra(False, spec, held)

    def give(piece):
        @pl.when(piece != me)
        def _():
            exchange(2, b_tx, b_ref, piece).start()

        @pl.when(piece == me)
        def _():
            b_ref[me] = b_tx[me]

    half = count // 2
    start = lax.rem(me // 2 + half // 2, half)
    for k in range(half):
        at = 2 * lax.rem(start + k, half)
        last = lax.rem(at + count - 1, count)
        backs = back_pair(inverse, [spec[1, at], spec[1, at + 1]])
        longs = back_pair(inverse, [spec[0, at], spec[0, at + 1]])
        for p in range(2):
            b_tx[at + p, 0:rows, :] = backs[p]
            b_tx[at + p, rows + TAIL : 2 * rows + TAIL, :] = longs[p]
        b_tx[at, rows : rows + TAIL, :] = backs[1][:TAIL]
        head = backs[0][:TAIL]
        b_tx[last, rows : rows + TAIL, :] = jnp.where(at == 0, jnp.zeros_like(head), head)
        if k > 0:
            give(last)
        give(at)
    give(lax.rem(2 * start + count - 1, count))

    for kind, source, target in ((1, y_tx, y_ref), (2, b_tx, b_ref)):
        for peer in peers:
            arrival(kind, source, target, peer).wait_recv()
    for kind, source, target in ((0, g_tx, g_rx), (1, y_tx, y_ref), (2, b_tx, b_ref)):
        for peer in peers:
            exchange(kind, source, target, peer).wait_send()
    edge.wait()

    @pl.when(me == count - 1)
    def _():
        edge_ref[...] = jnp.zeros_like(edge_ref)


def sum_kernel(part_ref, short_ref, skip_ref, one_rx, total, two_rx, sent, came):
    count = part_ref.shape[0]
    cw = part_ref.shape[2]
    tap_count = short_ref.shape[1]
    me = lax.axis_index("ctx")
    greet([("ctx", count)])
    peers = [lax.rem(me + o, count) for o in far_first(count)]

    def exchange(kind, source, target, peer):
        return send(source, target.at[me], sent.at[kind, peer], came.at[kind, me], peer)

    def arrival(kind, source, target, peer):
        return send(source, target.at[peer], sent.at[kind, peer], came.at[kind, peer], peer)

    for peer in peers:
        exchange(0, part_ref.at[peer], one_rx, peer).start()
    one_rx[me] = part_ref[me]
    for peer in peers:
        arrival(0, part_ref.at[peer], one_rx, peer).wait_recv()
    value = one_rx[0]
    for c in range(1, count):
        value = value + one_rx[c]
    total[...] = value
    for peer in peers:
        exchange(1, total, two_rx, peer).start()
    two_rx[me] = value
    for peer in peers:
        arrival(1, total, two_rx, peer).wait_recv()
    for c in range(count):
        lanes = slice(c * cw, (c + 1) * cw)
        for s in range(3):
            short_ref[s, :, lanes] = two_rx[c, s * tap_count : (s + 1) * tap_count, :]
        skip_ref[:, lanes] = two_rx[c, 3 * tap_count : 3 * tap_count + 1, :]
    for peer in peers:
        exchange(0, part_ref.at[peer], one_rx, peer).wait_send()
        exchange(1, total, two_rx, peer).wait_send()


def leave_kernel(pieces, q_ref, k_ref, v_ref, before, after, go_ref, go_after, taps, skip_ref,
                 y_ref, b_ref, dq_ref, dk_ref, dv_ref, long_ref, sums_ref, ext, go_ext, grad_ext):
    rows, width = q_ref.shape
    cw = width // pieces
    rim = taps.shape[1] - 1
    tap_count = taps.shape[1]
    more = rows + PAD
    sums_ref[...] = jnp.zeros_like(sums_ref)
    for c in range(pieces):
        lanes = slice(c * cw, (c + 1) * cw)
        filtered = []
        for s, ref in enumerate((q_ref, k_ref, v_ref)):
            fill(ext.at[s], before[s, TAIL - rim :, lanes], ref[:, lanes], after[s, 0:rim, lanes], rim)
            filtered.append(short(ext.at[s], taps, more, lanes, s))
        fill(go_ext, jnp.zeros((rim, cw), F32), go_ref[:, lanes], go_after[0:rim, lanes], rim)
        grad_o = go_ext[PAD : PAD + more, :]
        mixed = filtered[1] * filtered[2]
        grad_y = grad_o * filtered[0]
        gain = skip_ref[:, lanes]
        y_full = y_ref[c, 0:more, :].astype(F32) + gain * mixed
        at = rows + TAIL
        grad_mixed = b_ref[c, 0:more, :].astype(F32) + gain * grad_y
        grad_ext[0, 0:more, :] = grad_o * y_full
        grad_ext[1, 0:more, :] = grad_mixed * filtered[2]
        grad_ext[2, 0:more, :] = grad_mixed * filtered[1]
        long_ref[:, lanes] = b_ref[c, at : at + rows, :].astype(F32)
        for s, ref in enumerate((dq_ref, dk_ref, dv_ref)):
            total = None
            own = grad_ext[s, 0:rows, :]
            for j in range(tap_count):
                term = taps[s, j : j + 1, lanes] * grad_ext[s, j : j + rows, :]
                total = term if total is None else total + term
                stream = ext[s, PAD - j : PAD - j + rows, :]
                row = s * tap_count + j
                sums_ref[c, row : row + 1, :] = jnp.sum(own * stream, axis=0, keepdims=True)
            ref[:, lanes] = total.astype(BF16)
        row = 3 * tap_count
        sums_ref[c, row : row + 1, :] = jnp.sum(
            grad_y[0:rows] * mixed[0:rows], axis=0, keepdims=True
        )


def call(kernel, out_shape, scratch, *args, hbm=(), **params):
    vmem = pl.BlockSpec(memory_space=pltpu.VMEM)
    return pl.pallas_call(
        kernel,
        out_shape=out_shape,
        in_specs=[pl.BlockSpec(memory_space=pl.ANY) if i in hbm else vmem
                  for i in range(len(args))],
        out_specs=jax.tree.map(lambda _: vmem, out_shape),
        scratch_shapes=scratch,
        compiler_params=pltpu.CompilerParams(**PARAMS, **params),
    )(*args)


def per_device(queries, keys, values, long_filter, short_filters, skip, w_out, d_out):
    ctx = lax.axis_size("ctx")
    rows, width = queries.shape
    cw = width // ctx
    tap_count = short_filters.shape[1]
    parts = lax.axis_size("ch")
    cols = d_out.shape[1]
    halves = 2
    ext = pltpu.VMEM((rows + 4 * PAD, cw), F32)
    shape = jax.ShapeDtypeStruct
    dma = pltpu.SemaphoreType.DMA
    edge = shape((3, TAIL, width), BF16)
    pair = (ctx, 2, rows, cw)
    mh, grad_o, before, after = call(
        gather_kernel,
        (shape(pair, BF16), shape((rows, width), BF16), edge, edge),
        [ext, pltpu.VMEM(pair, BF16), pltpu.VMEM((parts, halves, rows, cols // halves), BF16),
         pltpu.VMEM((parts, width, cols), BF16), pltpu.VMEM((rows, width), F32),
         dma((6,)), dma((6,)), dma((ctx,)), dma((ctx,)), dma((parts // 2, halves)),
         dma((parts // 2, halves)), dma((parts, halves)), dma((parts,))],
        queries, keys, values, long_filter, short_filters, d_out, w_out,
        hbm=(6,), collective_id=3, has_side_effects=True,
    )
    forward, inverse = tables(rows)
    spare = ctx if ctx > 8 else 1
    one = shape((ctx, rows + TAIL, cw), BF16)
    two = shape((ctx, 2 * rows + TAIL, cw), BF16)
    piece = pltpu.VMEM((ctx, rows, cw), BF16)
    y, back, go_after = call(
        conv_kernel,
        (one, two, shape((TAIL, width), BF16)),
        [ext, piece, piece, pltpu.VMEM(one.shape, BF16), pltpu.VMEM(two.shape, BF16),
         pltpu.VMEM((3, ctx, 2 * rows, cw), F32), pltpu.VMEM((2, spare, 2, 8, cw), F32),
         pltpu.SemaphoreType.DMA((3, ctx)), pltpu.SemaphoreType.DMA((3, ctx)),
         pltpu.SemaphoreType.DMA((2,))],
        queries, before, grad_o, short_filters, mh, jnp.asarray(forward), jnp.asarray(inverse),
        collective_id=1, has_side_effects=True,
    )
    stream = shape((rows, width), BF16)
    dq, dk, dv, d_long, sums = call(
        functools.partial(leave_kernel, ctx),
        (stream, stream, stream, shape((rows, width), F32), shape((ctx, 16, cw), F32)),
        [pltpu.VMEM((3, rows + 4 * PAD, cw), F32), ext, pltpu.VMEM((3, rows + 4 * PAD, cw), F32)],
        queries, keys, values, before, after, grad_o, go_after, short_filters, skip[None], y, back,
    )
    small = pltpu.VMEM((ctx, 16, cw), F32)
    d_short, d_skip = call(
        sum_kernel,
        (shape((3, tap_count, width), F32), shape((1, width), F32)),
        [small, pltpu.VMEM((16, cw), F32), small,
         pltpu.SemaphoreType.DMA((2, ctx)), pltpu.SemaphoreType.DMA((2, ctx))],
        sums,
        collective_id=2, has_side_effects=True,
    )
    return dq, dk, dv, d_long, d_short, d_skip[0]


def solution(mesh):
    in_specs = (
        P("ctx", "ch"),
        P("ctx", "ch"),
        P("ctx", "ch"),
        P("ctx", "ch"),
        P(None, None, "ch"),
        P("ch"),
        P("ch", None),
        P("ctx", "ch"),
    )
    out_specs = (
        P("ctx", "ch"),
        P("ctx", "ch"),
        P("ctx", "ch"),
        P("ctx", "ch"),
        P(None, None, "ch"),
        P("ch"),
    )
    return jax.shard_map(
        per_device, mesh=mesh, in_specs=in_specs, out_specs=out_specs, check_vma=False
    )
```

profile of v0, /device:TPU:0, one launch (start us, length us, event | category | flops | bytes accessed | tf_op | source)
XLA Modules:
  0.0 118.2 jit_solution(6493785437932307448)
XLA Ops:
  0.6 35.6 %shard_map.145 = (bf16[8,2,256,128]{3,2,1,0:T(8,128)(2,1)}, bf16[256,1024]{1,0:T(8,128)(2,1)}, bf16[3,16,1024]{2,1,0:T(8,128)(2,1)}, bf16[3,16,1024]{2,1,0:T(8,128)(2,1)}) custom-call(bf16[256,1024]{1,0:T(8,128)(2,1)} %q_ref.5, bf16[256,1024]{1,0:T(8,128)(2,1)} %k_ref.3, bf16[256,1024]{1,0:T(8,128)(2,1)} %v_ref.3, f32[256,1024]{1,0:T(8,128)} %long_ref.1, ...), custom_call_target="tpu_custom_call" | custom-call | tf_op jit(solution)/shard_map/pallas_call | solution.py:490
  36.3 51.4 %shard_map.146 = (bf16[8,272,128]{2,1,0:T(8,128)(2,1)}, bf16[8,528,128]{2,1,0:T(8,128)(2,1)}, bf16[16,1024]{1,0:T(8,128)(2,1)}) custom-call(bf16[256,1024]{1,0:T(8,128)(2,1)} %q_ref.5, bf16[3,16,1024]{2,1,0:T(8,128)(2,1)} %get-tuple-element.20.before, bf16[256,1024]{1,0:T(8,128)(2,1)} %get-tuple-element.22.go_ref, f32[3,3,1024]{2,1,0:T(4,128)} %taps.5, ...), custom_call_target="tpu_custom_call" | custom-call | tf_op jit(solution)/shard_map/pallas_call | solution.py:490
  87.7 7.4 %shard_map.147 = (bf16[256,1024]{1,0:T(8,128)(2,1)}, bf16[256,1024]{1,0:T(8,128)(2,1)}, bf16[256,1024]{1,0:T(8,128)(2,1)}, f32[256,1024]{1,0:T(8,128)}, f32[8,16,128]{2,1,0:T(8,128)}) custom-call(bf16[256,1024]{1,0:T(8,128)(2,1)} %q_ref.5, bf16[256,1024]{1,0:T(8,128)(2,1)} %k_ref.3, bf16[256,1024]{1,0:T(8,128)(2,1)} %v_ref.3, ...), custom_call_target="tpu_custom_call" | custom-call | tf_op jit(solution)/shard_map/pallas_call | solution.py:490
  95.1 20.4 %shard_map.148 = (f32[3,3,1024]{2,1,0:T(4,128)}, f32[1,1024]{1,0:T(1,128)}) custom-call(f32[8,16,128]{2,1,0:T(8,128)} %get-tuple-element.31.part_ref), custom_call_target="tpu_custom_call" | custom-call | tf_op jit(solution)/shard_map/pallas_call | solution.py:490
  115.5 1.4 %copy.18 = f32[3,3,1024]{2,1,0:T(4,128)} copy(f32[3,3,1024]{2,1,0:T(4,128)} %get-tuple-element.44) | data formatting | bytes 73728
  116.9 1.3 %copy.19 = f32[1024]{0:T(1024)} copy(f32[1024]{0:T(1024)} %bitcast.3) | data formatting | bytes 8192
where the time goes:
time: 118 us
  Pallas kernels  115 us (97%)
  local copies, waits for them, and re-layouts  2.7 us (2%)
    pallas_call x4, Pallas kernels, call(): pl.pallas_call(kernel, out_shape=out_shape, in_specs=[pl.BlockSpec(memory...  115 us
    unnamed x2, local copies, waits for them, and re-layouts  2.7 us

commit v1 on v0

--- a/solution.py
+++ b/solution.py
@@ -1,5 +1,6 @@
 import functools
 import math
+import types
 
 import jax
 import jax.numpy as jnp
@@ -498,10 +499,476 @@
     )(*args)
 
 
+def whole_kernel(names, *refs):
+    s = types.SimpleNamespace(**dict(zip(names, refs)))
+    count, rows, cw = s.h_rx.shape
+    parts, pieces = s.held.shape[:2]
+    cols = s.d_own.shape[1]
+    piece = cols // pieces
+    tap_count = s.taps.shape[1]
+    rim = tap_count - 1
+    more = rows + PAD
+    me = lax.axis_index("ctx")
+    mine = lax.axis_index("ch")
+    partner = mine + 1 - 2 * lax.rem(mine, 2)
+    rest = [lax.rem(mine + 2 * o, parts) for o in range(1, parts // 2)]
+    other = [lax.rem(partner + 2 * o, parts) for o in range(1, parts // 2)]
+    after_me = lax.rem(me + 1, count)
+    before_me = lax.rem(me + count - 1, count)
+    peers = [lax.rem(me + o, count) for o in far_first(count)]
+    streams = (s.q_hbm, s.k_hbm, s.v_hbm)
+
+    def load(source, target, i):
+        return pltpu.make_async_copy(source, target, s.load_sem.at[i])
+
+    long_load = load(s.long_hbm, s.long_own, 0)
+    stream_loads = [load(streams[i], s.own.at[i], 1 + i) for i in range(3)]
+    d_load = load(s.d_hbm, s.d_own, 4)
+    table_loads = [load(s.fwd_hbm, s.fwd, 5), load(s.inv_hbm, s.inv, 6)]
+
+    def weight(part):
+        lanes = pl.ds(pl.multiple_of(part * cols, cols), cols)
+        return pltpu.make_async_copy(s.w_hbm.at[:, lanes], s.weights.at[part], s.w_sem.at[part])
+
+    long_load.start()
+    for i in (1, 2, 0):
+        stream_loads[i].start()
+    d_load.start()
+    weight(mine).start()
+    weight(partner).start()
+    for table in table_loads:
+        table.start()
+    for part in [p for pair in zip(rest, other) for p in pair]:
+        weight(part).start()
+
+    greet([("ctx", count), ("ch", parts)])
+
+    edges = []
+    for i in (1, 2, 0):
+        edges.append(send(streams[i].at[rows - TAIL : rows], s.before.at[i], s.edge_sent.at[i],
+                          s.edge_came.at[i], after_me))
+    for i in (1, 2, 0):
+        edges.append(send(streams[i].at[0:TAIL], s.after.at[i], s.edge_sent.at[3 + i],
+                          s.edge_came.at[3 + i], before_me))
+    for edge in edges:
+        edge.start()
+
+    def own(slot, p, peer):
+        lanes = slice(p * piece, (p + 1) * piece)
+        return send(s.d_hbm.at[:, lanes], s.held.at[mine, p], s.own_sent.at[slot, p],
+                    s.d_came.at[mine, p], peer, "ch")
+
+    def passed(slot, p, part):
+        return send(s.held.at[part, p], s.held.at[part, p], s.pass_sent.at[slot, p],
+                    s.d_came.at[part, p], partner, "ch")
+
+    for p in range(pieces):
+        for slot, peer in enumerate(rest + [partner]):
+            own(slot, p, peer).start()
+
+    def exchange(kind, source, target, peer):
+        return send(source.at[peer], target.at[me], s.sent.at[kind, peer], s.came.at[kind, me],
+                    peer)
+
+    def arrival(kind, source, target, peer):
+        return send(source.at[peer], target.at[peer], s.sent.at[kind, peer],
+                    s.came.at[kind, peer], peer)
+
+    def arrive(kind, source, target):
+        for peer in peers:
+            arrival(kind, source, target, peer).wait_recv()
+
+    def chunk(c):
+        return pl.ds(pl.multiple_of(c * cw, cw), cw)
+
+    def filtered(i, lanes):
+        total = None
+        for j in range(tap_count):
+            term = s.taps[i, j : j + 1, lanes] * s.ext[i, PAD - j : PAD - j + more, lanes]
+            total = term if total is None else total + term
+        return total
+
+    def fill_own(i):
+        def body(c, carry):
+            lanes = chunk(c)
+            s.ext[i, 0:PAD, lanes] = jnp.zeros((PAD, cw), F32)
+            s.ext[i, PAD + rows :, lanes] = jnp.zeros((3 * PAD, cw), F32)
+            s.ext[i, PAD : PAD + rows, lanes] = s.own[i, :, lanes].astype(F32)
+            return carry
+
+        lax.fori_loop(0, count, body, 0)
+
+    def fill_rim(i):
+        s.ext[i, PAD - rim : PAD, :] = s.before[i, TAIL - rim :, :].astype(F32)
+        s.ext[i, PAD + rows : PAD + rows + rim, :] = s.after[i, 0:rim, :].astype(F32)
+
+    long_load.wait()
+    for peer in peers + [me]:
+        s.h_tx[peer] = s.long_own[:, chunk(peer)].astype(BF16)
+        if peer is not me:
+            exchange(0, s.h_tx, s.h_rx, peer).start()
+    s.h_rx[me] = s.h_tx[me]
+
+    for i in (1, 2, 0):
+        stream_loads[i].wait()
+        fill_own(i)
+    for edge in edges:
+        edge.wait()
+
+    @pl.when(me == 0)
+    def _():
+        s.before[...] = jnp.zeros_like(s.before)
+
+    @pl.when(me == count - 1)
+    def _():
+        s.after[...] = jnp.zeros_like(s.after)
+
+    for i in (1, 2, 0):
+        fill_rim(i)
+    for peer in peers + [me]:
+        lanes = chunk(peer)
+        keyed = filtered(1, lanes)
+        valued = filtered(2, lanes)
+        s.filt[1, :, lanes] = keyed
+        s.filt[2, :, lanes] = valued
+        s.m_tx[peer] = (keyed[0:rows] * valued[0:rows]).astype(BF16)
+        if peer is not me:
+            exchange(1, s.m_tx, s.m_rx, peer).start()
+    s.m_rx[me] = s.m_tx[me]
+
+    def query(c, carry):
+        s.filt[0, :, chunk(c)] = filtered(0, chunk(c))
+        return carry
+
+    lax.fori_loop(0, count, query, 0)
+
+    def product(data, part, p=None):
+        lanes = slice(None) if p is None else slice(p * piece, (p + 1) * piece)
+        return lax.dot_general(data, s.weights[part, :, lanes], (((1,), (1,)), ((), ())),
+                               preferred_element_type=F32)
+
+    def take(part, p):
+        s.total[...] += product(s.held[part, p], part, p)
+
+    d_load.wait()
+    weight(mine).wait()
+    s.total[...] = product(s.d_own[...], mine)
+    weight(partner).wait()
+    for p in range(pieces):
+        passed(0, p, partner).wait_recv()
+        take(partner, p)
+
+    def relay(slot, direct, relayed, p):
+        passed(slot, p, direct).wait_recv()
+        passed(slot, p, direct).start()
+        take(direct, p)
+        passed(slot, p, relayed).wait_recv()
+        take(relayed, p)
+
+    steps = [(slot, pair, p) for slot, pair in enumerate(zip(rest, other)) for p in range(pieces)]
+    for direct, relayed in zip(rest, other):
+        weight(direct).wait()
+        weight(relayed).wait()
+    for table in table_loads:
+        table.wait()
+    for at, (slot, (direct, relayed), p) in enumerate(steps):
+        if at == len(steps) // 2:
+            arrive(0, s.h_tx, s.h_rx)
+            spectra(s.fwd, [(s.h_rx.at[i], 1, i) for i in range(count)], s.spec)
+        relay(slot, direct, relayed, p)
+    if not steps:
+        arrive(0, s.h_tx, s.h_rx)
+        spectra(s.fwd, [(s.h_rx.at[i], 1, i) for i in range(count)], s.spec)
+
+    s.go_head[...] = s.total[0:TAIL, :].astype(BF16)
+    edge = send(s.go_head, s.go_after, s.edge_sent.at[6], s.edge_came.at[6], before_me)
+    edge.start()
+    for peer in peers + [me]:
+        lanes = chunk(peer)
+        value = s.total[:, lanes].astype(BF16).astype(F32)
+        s.go[0:rows, lanes] = value
+        s.g_tx[peer] = (value * s.filt[0, 0:rows, lanes]).astype(BF16)
+        if peer is not me:
+            exchange(2, s.g_tx, s.g_rx, peer).start()
+    s.g_rx[me] = s.g_tx[me]
+
+    half = count // 2
+    start = lax.rem(me // 2 + half // 2, half)
+
+    def give(kind, source, target, to):
+        @pl.when(to != me)
+        def _():
+            exchange(kind, source, target, to).start()
+
+    def deliver(kind, source, target, at_spec, tail):
+        for k in range(half):
+            at = 2 * lax.rem(start + k, half)
+            last = lax.rem(at + count - 1, count)
+            out = back_pair(s.inv, [s.spec[at_spec, at], s.spec[at_spec, at + 1]])
+            for p in range(2):
+                source[at + p, 0:rows, :] = out[p]
+            if not tail:
+                give(kind, source, target, at)
+                give(kind, source, target, at + 1)
+                continue
+            head = out[0][:TAIL]
+            source[at, rows : rows + TAIL, :] = out[1][:TAIL]
+            source[last, rows : rows + TAIL, :] = jnp.where(at == 0, jnp.zeros_like(head), head)
+            if k > 0:
+                give(kind, source, target, last)
+            give(kind, source, target, at)
+        if tail:
+            give(kind, source, target, lax.rem(2 * start + count - 1, count))
+
+    arrive(1, s.m_tx, s.m_rx)
+    spectra(s.fwd, [(s.m_rx.at[i], 0, i) for i in range(count)], s.spec)
+    mix(s.spec, "y")
+    deliver(3, s.y_tx, s.y_rx, 2, True)
+    s.y_rx[me] = s.y_tx[me]
+
+    arrive(2, s.g_tx, s.g_rx)
+    spectra(s.fwd, [(s.g_rx.at[i], 2, i) for i in range(count)], s.spec)
+    mix(s.spec, "b")
+    deliver(4, s.b_tx, s.b_rx, 1, True)
+    s.b_rx[me] = s.b_tx[me]
+    mix(s.spec, "l")
+    deliver(5, s.l_tx, s.l_hbm, 0, False)
+    l_own = pltpu.make_async_copy(s.l_tx.at[me], s.l_hbm.at[me], s.out_sem.at[3])
+    l_own.start()
+
+    edge.wait()
+
+    @pl.when(me == count - 1)
+    def _():
+        s.go_after[...] = jnp.zeros_like(s.go_after)
+
+    s.go[rows:, :] = jnp.zeros_like(s.go[rows:, :])
+    s.go[rows : rows + rim, :] = s.go_after[0:rim, :].astype(F32)
+
+    def finish(i, c, lanes, grad):
+        s.grad[i, 0:more, :] = grad
+        own_rows = grad[0:rows]
+        total = None
+        for j in range(tap_count):
+            term = s.taps[i, j : j + 1, lanes] * s.grad[i, j : j + rows, :]
+            total = term if total is None else total + term
+            stream = s.ext[i, PAD - j : PAD - j + rows, lanes]
+            row = i * tap_count + j
+            s.part[c, row : row + 1, :] = jnp.sum(own_rows * stream, axis=0, keepdims=True)
+        s.done[i, :, lanes] = total.astype(BF16)
+
+    def first_half(c, carry):
+        lanes = chunk(c)
+        mixed = s.filt[1, :, lanes] * s.filt[2, :, lanes]
+        grad_o = s.go[:, lanes]
+        grad_y = grad_o * s.filt[0, :, lanes]
+        row = 3 * tap_count
+        s.part[c, row:, :] = jnp.zeros((16 - row, cw), F32)
+        s.part[c, row : row + 1, :] = jnp.sum(grad_y[0:rows] * mixed[0:rows], axis=0, keepdims=True)
+        y_full = s.y_rx[c, 0:more, :].astype(F32) + s.skip[:, lanes] * mixed
+        finish(0, c, lanes, grad_o * y_full)
+        return carry
+
+    def second_half(c, carry):
+        lanes = chunk(c)
+        grad_y = s.go[:, lanes] * s.filt[0, :, lanes]
+        grad_mixed = s.b_rx[c, 0:more, :].astype(F32) + s.skip[:, lanes] * grad_y
+        finish(1, c, lanes, grad_mixed * s.filt[2, :, lanes])
+        finish(2, c, lanes, grad_mixed * s.filt[1, :, lanes])
+        return carry
+
+    outs = [pltpu.make_async_copy(s.done.at[i], ref, s.out_sem.at[i])
+            for i, ref in enumerate((s.dq_hbm, s.dk_hbm, s.dv_hbm))]
+    arrive(3, s.y_tx, s.y_rx)
+    lax.fori_loop(0, count, first_half, 0)
+    outs[0].start()
+    arrive(4, s.b_tx, s.b_rx)
+    lax.fori_loop(0, count, second_half, 0)
+
+    for peer in peers:
+        exchange(6, s.part, s.one_rx, peer).start()
+    outs[1].start()
+    outs[2].start()
+    s.one_rx[me] = s.part[me]
+    arrive(6, s.part, s.one_rx)
+    value = s.one_rx[0]
+    for c in range(1, count):
+        value = value + s.one_rx[c]
+    s.sum[...] = value
+
+    def spread(peer):
+        return send(s.sum, s.sums_hbm.at[me], s.sent.at[7, peer], s.came.at[7, me], peer)
+
+    for peer in peers:
+        spread(peer).start()
+    sums_own = pltpu.make_async_copy(s.sum, s.sums_hbm.at[me], s.out_sem.at[4])
+    sums_own.start()
+
+    for peer in peers:
+        send(s.sum, s.sums_hbm.at[peer], s.sent.at[7, peer], s.came.at[7, peer], peer).wait_recv()
+    arrive(5, s.l_tx, s.l_hbm)
+    for copy in outs + [l_own, sums_own]:
+        copy.wait()
+    sends = ((s.h_tx, s.h_rx), (s.m_tx, s.m_rx), (s.g_tx, s.g_rx), (s.y_tx, s.y_rx),
+             (s.b_tx, s.b_rx), (s.l_tx, s.l_hbm), (s.part, s.one_rx))
+    for kind, (source, target) in enumerate(sends):
+        for peer in peers:
+            exchange(kind, source, target, peer).wait_send()
+    for peer in peers:
+        spread(peer).wait_send()
+    for p in range(pieces):
+        for slot, peer in enumerate(rest + [partner]):
+            own(slot, p, peer).wait_send()
+        for slot, direct in enumerate(rest):
+            passed(slot, p, direct).wait_send()
+
+
+def mix(spec, what):
+    count, rows2, cw = spec.shape[1:]
+    half = rows2 // 2
+    step = 8
+    sign = 1.0 - 2.0 * (lax.broadcasted_iota(jnp.int32, (step, cw), 0) % 2).astype(F32)
+
+    def primes(blocks):
+        out = [blocks[0]]
+        for d in range(1, count):
+            re, im = blocks[d]
+            old_re, old_im = blocks[d - 1]
+            out.append((re - sign * old_im, im + sign * old_re))
+        return out
+
+    def chunk(r, carry):
+        low = pl.ds(pl.multiple_of(r * step, step), step)
+        high = pl.ds(pl.multiple_of(half + r * step, step), step)
+
+        def load(s, i):
+            return spec[s, i, low, :], spec[s, i, high, :]
+
+        def save(s, i, value):
+            spec[s, i, low, :] = value[0]
+            spec[s, i, high, :] = value[1]
+
+        if what == "y":
+            taps = primes([load(1, i) for i in range(count)])
+            for i in range(count):
+                save(1, i, taps[i])
+            mixed = [load(0, i) for i in range(count)]
+            for i in range(count):
+                total = None
+                for d in range(i + 1):
+                    total = add(total, times(taps[d], mixed[i - d]))
+                save(2, i, total)
+            return carry
+        s = 1 if what == "b" else 0
+        taps = [load(s, i) for i in range(count)]
+        if what == "l":
+            taps = primes(taps)
+        grads = [load(2, i) for i in range(count)]
+        for b in range(count):
+            total = None
+            for e in range(count - b):
+                total = add(total, conj_times(taps[e], grads[b + e]))
+            save(s, b, total)
+        return carry
+
+    lax.fori_loop(0, half // step, chunk, 0)
+
+
+def result_kernel(dq_in, dk_in, dv_in, l_ref, sums_ref,
+                  dq_out, dk_out, dv_out, long_ref, short_ref, skip_ref, sem):
+    count, rows, cw = l_ref.shape
+    tap_count = short_ref.shape[1]
+    pairs = ((dq_in, dq_out), (dk_in, dk_out), (dv_in, dv_out))
+    copies = [pltpu.make_async_copy(a, b, sem.at[i]) for i, (a, b) in enumerate(pairs)]
+    for copy in copies:
+        copy.start()
+    for c in range(count):
+        lanes = slice(c * cw, (c + 1) * cw)
+        long_ref[:, lanes] = l_ref[c].astype(F32)
+        for i in range(3):
+            short_ref[i, :, lanes] = sums_ref[c, i * tap_count : (i + 1) * tap_count, :]
+        skip_ref[:, lanes] = sums_ref[c, 3 * tap_count : 3 * tap_count + 1, :]
+    for copy in copies:
+        copy.wait()
+
+
+def joined(queries, keys, values, long_filter, short_filters, skip, w_out, d_out):
+    ctx = lax.axis_size("ctx")
+    parts = lax.axis_size("ch")
+    rows, width = queries.shape
+    cw = width // ctx
+    tap_count = short_filters.shape[1]
+    cols = d_out.shape[1]
+    pieces = 4
+    shape = jax.ShapeDtypeStruct
+    dma = pltpu.SemaphoreType.DMA
+    forward, inverse = (jnp.asarray(t) for t in tables(rows))
+    anyw = pl.BlockSpec(memory_space=pl.ANY)
+    vmem = pl.BlockSpec(memory_space=pltpu.VMEM)
+    inputs = [
+        ("q_hbm", queries, anyw), ("k_hbm", keys, anyw), ("v_hbm", values, anyw),
+        ("long_hbm", long_filter, anyw), ("taps", short_filters, vmem),
+        ("skip", skip[None], vmem), ("d_hbm", d_out, anyw), ("w_hbm", w_out, anyw),
+        ("fwd_hbm", forward, anyw), ("inv_hbm", inverse, anyw),
+    ]
+    stream = shape((rows, width), BF16)
+    outputs = [
+        ("dq_hbm", stream), ("dk_hbm", stream), ("dv_hbm", stream),
+        ("l_hbm", shape((ctx, rows, cw), BF16)), ("sums_hbm", shape((ctx, 16, cw), F32)),
+    ]
+    bulk = pltpu.VMEM((ctx, rows, cw), BF16)
+    tailed = pltpu.VMEM((ctx, rows + TAIL, cw), BF16)
+    small = pltpu.VMEM((ctx, 16, cw), F32)
+    rim = pltpu.VMEM((3, TAIL, width), BF16)
+    scratch = [
+        ("long_own", pltpu.VMEM((rows, width), F32)), ("own", pltpu.VMEM((3, rows, width), BF16)),
+        ("d_own", pltpu.VMEM((rows, cols), BF16)), ("fwd", pltpu.VMEM(forward.shape, BF16)),
+        ("inv", pltpu.VMEM(inverse.shape, BF16)), ("before", rim), ("after", rim),
+        ("ext", pltpu.VMEM((3, rows + 4 * PAD, width), F32)),
+        ("filt", pltpu.VMEM((3, rows + PAD, width), F32)),
+        ("held", pltpu.VMEM((parts, pieces, rows, cols // pieces), BF16)),
+        ("weights", pltpu.VMEM((parts, width, cols), BF16)),
+        ("total", pltpu.VMEM((rows, width), F32)),
+        ("go", pltpu.VMEM((rows + PAD, width), F32)),
+        ("go_head", pltpu.VMEM((TAIL, width), BF16)), ("go_after", pltpu.VMEM((TAIL, width), BF16)),
+        ("h_tx", bulk), ("h_rx", bulk), ("m_tx", bulk), ("m_rx", bulk), ("g_tx", bulk),
+        ("g_rx", bulk), ("y_tx", tailed), ("y_rx", tailed), ("b_tx", tailed), ("b_rx", tailed),
+        ("l_tx", bulk), ("spec", pltpu.VMEM((3, ctx, 2 * rows, cw), F32)),
+        ("grad", pltpu.VMEM((3, rows + 4 * PAD, cw), F32)),
+        ("done", pltpu.VMEM((3, rows, width), BF16)),
+        ("part", small), ("one_rx", small), ("sum", pltpu.VMEM((16, cw), F32)),
+        ("load_sem", dma((7,))), ("w_sem", dma((parts,))), ("edge_sent", dma((7,))),
+        ("edge_came", dma((7,))), ("own_sent", dma((parts // 2, pieces))),
+        ("pass_sent", dma((parts // 2, pieces))), ("d_came", dma((parts, pieces))),
+        ("sent", dma((8, ctx))), ("came", dma((8, ctx))), ("out_sem", dma((5,))),
+    ]
+    names = tuple(name for name, *_ in inputs + outputs + scratch)
+    dq, dk, dv, back, sums = pl.pallas_call(
+        functools.partial(whole_kernel, names),
+        out_shape=[out for _, out in outputs],
+        in_specs=[spec for _, _, spec in inputs],
+        out_specs=[anyw] * len(outputs),
+        scratch_shapes=[kind for _, kind in scratch],
+        compiler_params=pltpu.CompilerParams(**PARAMS, collective_id=0, has_side_effects=True),
+    )(*[value for _, value, _ in inputs])
+    dq, dk, dv, d_long, d_short, d_skip = pl.pallas_call(
+        result_kernel,
+        out_shape=[stream, stream, stream, shape((rows, width), F32),
+                   shape((3, tap_count, width), F32), shape((1, width), F32)],
+        in_specs=[anyw, anyw, anyw, vmem, vmem],
+        out_specs=[anyw, anyw, anyw, vmem, vmem, vmem],
+        scratch_shapes=[dma((3,))],
+        compiler_params=pltpu.CompilerParams(**PARAMS),
+    )(dq, dk, dv, back, sums)
+    return dq, dk, dv, d_long, d_short, d_skip[0]
+
+
 def per_device(queries, keys, values, long_filter, short_filters, skip, w_out, d_out):
     ctx = lax.axis_size("ctx")
     rows, width = queries.shape
     cw = width // ctx
+    if cw % 128 == 0 and ctx <= 8:
+        return joined(queries, keys, values, long_filter, short_filters, skip, w_out, d_out)
     tap_count = short_filters.shape[1]
     parts = lax.axis_size("ch")
     cols = d_out.shape[1]

time: 118 us -> 141 us (1.19)
  Pallas kernels: 115 us -> 141 us
  local copies, waits for them, and re-layouts: 2.7 us -> 0 us
    pallas_call x4 -> x2, Pallas kernels: 115 us -> 141 us  [the longest x1 89.8 us: joined(): pl.pallas_call(functools.partial(whole_kernel, names), out_shape=[out for...]
    unnamed x2 -> x0, local copies, waits for them, and re-layouts: 2.7 us -> none
where the time goes in v1:
time: 141 us
  Pallas kernels  141 us (100%)
    pallas_call x1, Pallas kernels, joined(): pl.pallas_call(functools.partial(whole_kernel, names), out_shape=[out for...  89.8 us
    pallas_call x1, Pallas kernels, joined(): pl.pallas_call(result_kernel, out_shape=[stream, stream, stream, shape((r...  50.8 us

profile of v1, /device:TPU:0, one launch (start us, length us, event | category | flops | bytes accessed | tf_op | source)
XLA Modules:
  0.0 141.3 jit_solution(18268128325872273996)
XLA Ops:
  0.6 89.8 %shard_map.145 = (bf16[256,1024]{1,0:T(8,128)(2,1)}, bf16[256,1024]{1,0:T(8,128)(2,1)}, bf16[256,1024]{1,0:T(8,128)(2,1)}, bf16[8,256,128]{2,1,0:T(8,128)(2,1)}, f32[8,16,128]{2,1,0:T(8,128)}) custom-call(bf16[256,1024]{1,0:T(8,128)(2,1)} %refs_0_.1, bf16[256,1024]{1,0:T(8,128)(2,1)} %refs_1_.1, bf16[256,1024]{1,0:T(8,128)(2,1)} %refs_2_.1, ...), custom_call_target="tpu_custom_call" | custom-call | tf_op jit(solution)/shard_map/pallas_call | solution.py:946
  90.5 50.8 %shard_map.146 = (bf16[256,1024]{1,0:T(8,128)(2,1)}, bf16[256,1024]{1,0:T(8,128)(2,1)}, bf16[256,1024]{1,0:T(8,128)(2,1)}, f32[256,1024]{1,0:T(8,128)}, f32[3,3,1024]{2,1,0:T(4,128)}, /*index=5*/f32[1,1024]{1,0:T(1,128)}) custom-call(bf16[256,1024]{1,0:T(8,128)(2,1)} %get-tuple-element.17.dq_in, bf16[256,1024]{1,0:T(8,128)(2,1)} %get-tuple-element.18.dk_in, ...), custom_call_target="tpu_custom_call" | custom-call | tf_op jit(solution)/shard_map/pallas_call | solution.py:954

commit v2 on v1

--- a/solution.py
+++ b/solution.py
@@ -502,12 +502,11 @@
 def whole_kernel(names, *refs):
     s = types.SimpleNamespace(**dict(zip(names, refs)))
     count, rows, cw = s.h_rx.shape
-    parts, pieces = s.held.shape[:2]
+    parts, _, pieces, tall, _ = s.held.shape
     cols = s.d_own.shape[1]
     piece = cols // pieces
     tap_count = s.taps.shape[1]
     rim = tap_count - 1
-    more = rows + PAD
     me = lax.axis_index("ctx")
     mine = lax.axis_index("ch")
     partner = mine + 1 - 2 * lax.rem(mine, 2)
@@ -547,24 +546,23 @@
     for i in (1, 2, 0):
         edges.append(send(streams[i].at[rows - TAIL : rows], s.before.at[i], s.edge_sent.at[i],
                           s.edge_came.at[i], after_me))
-    for i in (1, 2, 0):
-        edges.append(send(streams[i].at[0:TAIL], s.after.at[i], s.edge_sent.at[3 + i],
-                          s.edge_came.at[3 + i], before_me))
     for edge in edges:
         edge.start()
 
-    def own(slot, p, peer):
-        lanes = slice(p * piece, (p + 1) * piece)
-        return send(s.d_hbm.at[:, lanes], s.held.at[mine, p], s.own_sent.at[slot, p],
-                    s.d_came.at[mine, p], peer, "ch")
-
-    def passed(slot, p, part):
-        return send(s.held.at[part, p], s.held.at[part, p], s.pass_sent.at[slot, p],
-                    s.d_came.at[part, p], partner, "ch")
-
-    for p in range(pieces):
+    batches = [(h, p) for h in range(rows // tall) for p in range(pieces)]
+
+    def own(slot, h, p, peer):
+        part = s.d_hbm.at[h * tall : (h + 1) * tall, p * piece : (p + 1) * piece]
+        return send(part, s.held.at[mine, h, p], s.own_sent.at[slot, h, p],
+                    s.d_came.at[mine, h, p], peer, "ch")
+
+    def passed(slot, h, p, part):
+        return send(s.held.at[part, h, p], s.held.at[part, h, p], s.pass_sent.at[slot, h, p],
+                    s.d_came.at[part, h, p], partner, "ch")
+
+    for h, p in batches:
         for slot, peer in enumerate(rest + [partner]):
-            own(slot, p, peer).start()
+            own(slot, h, p, peer).start()
 
     def exchange(kind, source, target, peer):
         return send(source.at[peer], target.at[me], s.sent.at[kind, peer], s.came.at[kind, me],
@@ -584,7 +582,7 @@
     def filtered(i, lanes):
         total = None
         for j in range(tap_count):
-            term = s.taps[i, j : j + 1, lanes] * s.ext[i, PAD - j : PAD - j + more, lanes]
+            term = s.taps[i, j : j + 1, lanes] * s.ext[i, PAD - j : PAD - j + rows, lanes]
             total = term if total is None else total + term
         return total
 
@@ -592,7 +590,6 @@
         def body(c, carry):
             lanes = chunk(c)
             s.ext[i, 0:PAD, lanes] = jnp.zeros((PAD, cw), F32)
-            s.ext[i, PAD + rows :, lanes] = jnp.zeros((3 * PAD, cw), F32)
             s.ext[i, PAD : PAD + rows, lanes] = s.own[i, :, lanes].astype(F32)
             return carry
 
@@ -600,7 +597,6 @@
 
     def fill_rim(i):
         s.ext[i, PAD - rim : PAD, :] = s.before[i, TAIL - rim :, :].astype(F32)
-        s.ext[i, PAD + rows : PAD + rows + rim, :] = s.after[i, 0:rim, :].astype(F32)
 
     long_load.wait()
     for peer in peers + [me]:
@@ -618,10 +614,6 @@
     @pl.when(me == 0)
     def _():
         s.before[...] = jnp.zeros_like(s.before)
-
-    @pl.when(me == count - 1)
-    def _():
-        s.after[...] = jnp.zeros_like(s.after)
 
     for i in (1, 2, 0):
         fill_rim(i)
@@ -631,7 +623,7 @@
         valued = filtered(2, lanes)
         s.filt[1, :, lanes] = keyed
         s.filt[2, :, lanes] = valued
-        s.m_tx[peer] = (keyed[0:rows] * valued[0:rows]).astype(BF16)
+        s.m_tx[peer] = (keyed * valued).astype(BF16)
         if peer is not me:
             exchange(1, s.m_tx, s.m_rx, peer).start()
     s.m_rx[me] = s.m_tx[me]
@@ -647,148 +639,167 @@
         return lax.dot_general(data, s.weights[part, :, lanes], (((1,), (1,)), ((), ())),
                                preferred_element_type=F32)
 
-    def take(part, p):
-        s.total[...] += product(s.held[part, p], part, p)
+    def take(part, h, p):
+        s.total[h * tall : (h + 1) * tall, :] += product(s.held[part, h, p], part, p)
+
+    def g_send(h, source, target, peer, slot):
+        at = slice(h * tall, (h + 1) * tall)
+        return send(source.at[peer, at], target.at[slot, at], s.g_sent.at[h, peer],
+                    s.g_came.at[h, slot], peer)
+
+    def gradient(h):
+        at = slice(h * tall, (h + 1) * tall)
+        for peer in peers + [me]:
+            lanes = chunk(peer)
+            value = s.total[at, lanes].astype(BF16).astype(F32)
+            s.go[at, lanes] = value
+            s.g_tx[peer, at, :] = (value * s.filt[0, at, lanes]).astype(BF16)
+            if peer is not me:
+                g_send(h, s.g_tx, s.g_rx, peer, me).start()
+        s.g_rx[me, at, :] = s.g_tx[me, at, :]
+
+    def long_spectra():
+        arrive(0, s.h_tx, s.h_rx)
+        spectra(s.fwd, [(s.h_rx.at[i], 1, i) for i in range(count)], s.spec)
 
     d_load.wait()
     weight(mine).wait()
     s.total[...] = product(s.d_own[...], mine)
     weight(partner).wait()
-    for p in range(pieces):
-        passed(0, p, partner).wait_recv()
-        take(partner, p)
-
-    def relay(slot, direct, relayed, p):
-        passed(slot, p, direct).wait_recv()
-        passed(slot, p, direct).start()
-        take(direct, p)
-        passed(slot, p, relayed).wait_recv()
-        take(relayed, p)
-
-    steps = [(slot, pair, p) for slot, pair in enumerate(zip(rest, other)) for p in range(pieces)]
+    for h, p in batches:
+        passed(0, h, p, partner).wait_recv()
+        take(partner, h, p)
     for direct, relayed in zip(rest, other):
         weight(direct).wait()
         weight(relayed).wait()
     for table in table_loads:
         table.wait()
-    for at, (slot, (direct, relayed), p) in enumerate(steps):
-        if at == len(steps) // 2:
-            arrive(0, s.h_tx, s.h_rx)
-            spectra(s.fwd, [(s.h_rx.at[i], 1, i) for i in range(count)], s.spec)
-        relay(slot, direct, relayed, p)
-    if not steps:
-        arrive(0, s.h_tx, s.h_rx)
-        spectra(s.fwd, [(s.h_rx.at[i], 1, i) for i in range(count)], s.spec)
-
-    s.go_head[...] = s.total[0:TAIL, :].astype(BF16)
-    edge = send(s.go_head, s.go_after, s.edge_sent.at[6], s.edge_came.at[6], before_me)
-    edge.start()
-    for peer in peers + [me]:
-        lanes = chunk(peer)
-        value = s.total[:, lanes].astype(BF16).astype(F32)
-        s.go[0:rows, lanes] = value
-        s.g_tx[peer] = (value * s.filt[0, 0:rows, lanes]).astype(BF16)
-        if peer is not me:
-            exchange(2, s.g_tx, s.g_rx, peer).start()
-    s.g_rx[me] = s.g_tx[me]
+    for h in range(rows // tall):
+        for p in range(pieces):
+            for slot, (direct, relayed) in enumerate(zip(rest, other)):
+                passed(slot, h, p, direct).wait_recv()
+                passed(slot, h, p, direct).start()
+                take(direct, h, p)
+                passed(slot, h, p, relayed).wait_recv()
+                take(relayed, h, p)
+        gradient(h)
+        if h == 0:
+            long_spectra()
 
     half = count // 2
     start = lax.rem(me // 2 + half // 2, half)
 
-    def give(kind, source, target, to):
+    def give_b(to):
         @pl.when(to != me)
         def _():
-            exchange(kind, source, target, to).start()
-
-    def deliver(kind, source, target, at_spec, tail):
+            exchange(4, s.b_tx, s.b_rx, to).start()
+
+    def keep(to):
+        pass
+
+    def deliver(give, source, at_spec):
         for k in range(half):
             at = 2 * lax.rem(start + k, half)
-            last = lax.rem(at + count - 1, count)
             out = back_pair(s.inv, [s.spec[at_spec, at], s.spec[at_spec, at + 1]])
             for p in range(2):
-                source[at + p, 0:rows, :] = out[p]
-            if not tail:
-                give(kind, source, target, at)
-                give(kind, source, target, at + 1)
-                continue
-            head = out[0][:TAIL]
-            source[at, rows : rows + TAIL, :] = out[1][:TAIL]
-            source[last, rows : rows + TAIL, :] = jnp.where(at == 0, jnp.zeros_like(head), head)
-            if k > 0:
-                give(kind, source, target, last)
-            give(kind, source, target, at)
-        if tail:
-            give(kind, source, target, lax.rem(2 * start + count - 1, count))
+                source[at + p] = out[p]
+                give(at + p)
 
     arrive(1, s.m_tx, s.m_rx)
     spectra(s.fwd, [(s.m_rx.at[i], 0, i) for i in range(count)], s.spec)
     mix(s.spec, "y")
-    deliver(3, s.y_tx, s.y_rx, 2, True)
+    deliver(keep, s.y_tx, 2)
     s.y_rx[me] = s.y_tx[me]
 
-    arrive(2, s.g_tx, s.g_rx)
+    for h in range(rows // tall):
+        for peer in peers:
+            g_send(h, s.g_tx, s.g_rx, peer, peer).wait_recv()
+    for peer in peers:
+        exchange(3, s.y_tx, s.y_rx, peer).start()
     spectra(s.fwd, [(s.g_rx.at[i], 2, i) for i in range(count)], s.spec)
     mix(s.spec, "b")
-    deliver(4, s.b_tx, s.b_rx, 1, True)
+    deliver(give_b, s.b_tx, 1)
     s.b_rx[me] = s.b_tx[me]
     mix(s.spec, "l")
-    deliver(5, s.l_tx, s.l_hbm, 0, False)
+    deliver(keep, s.l_tx, 0)
     l_own = pltpu.make_async_copy(s.l_tx.at[me], s.l_hbm.at[me], s.out_sem.at[3])
     l_own.start()
 
-    edge.wait()
-
-    @pl.when(me == count - 1)
-    def _():
-        s.go_after[...] = jnp.zeros_like(s.go_after)
-
-    s.go[rows:, :] = jnp.zeros_like(s.go[rows:, :])
-    s.go[rows : rows + rim, :] = s.go_after[0:rim, :].astype(F32)
-
     def finish(i, c, lanes, grad):
-        s.grad[i, 0:more, :] = grad
-        own_rows = grad[0:rows]
+        s.grad[i, 0:rows, :] = grad
+        s.grad[i, rows:, :] = jnp.zeros((PAD, cw), F32)
+        s.head_tx[i, :, lanes] = grad[0:PAD]
+        s.tail[i, 0:TAIL, lanes] = grad[rows - TAIL :]
         total = None
         for j in range(tap_count):
             term = s.taps[i, j : j + 1, lanes] * s.grad[i, j : j + rows, :]
             total = term if total is None else total + term
             stream = s.ext[i, PAD - j : PAD - j + rows, lanes]
             row = i * tap_count + j
-            s.part[c, row : row + 1, :] = jnp.sum(own_rows * stream, axis=0, keepdims=True)
+            s.part[c, row : row + 1, :] = jnp.sum(grad * stream, axis=0, keepdims=True)
         s.done[i, :, lanes] = total.astype(BF16)
 
     def first_half(c, carry):
         lanes = chunk(c)
         mixed = s.filt[1, :, lanes] * s.filt[2, :, lanes]
         grad_o = s.go[:, lanes]
-        grad_y = grad_o * s.filt[0, :, lanes]
         row = 3 * tap_count
         s.part[c, row:, :] = jnp.zeros((16 - row, cw), F32)
-        s.part[c, row : row + 1, :] = jnp.sum(grad_y[0:rows] * mixed[0:rows], axis=0, keepdims=True)
-        y_full = s.y_rx[c, 0:more, :].astype(F32) + s.skip[:, lanes] * mixed
+        s.part[c, row : row + 1, :] = jnp.sum(
+            grad_o * s.filt[0, :, lanes] * mixed, axis=0, keepdims=True
+        )
+        y_full = s.y_rx[c].astype(F32) + s.skip[:, lanes] * mixed
         finish(0, c, lanes, grad_o * y_full)
         return carry
 
-    def second_half(c, carry):
+    def second_half(k, carry):
+        middle = count // 2
+        c = lax.rem(me + count - middle + (2 * lax.rem(k, 2) - 1) * ((k + 1) // 2), count)
+
+        @pl.when(c != me)
+        def _():
+            arrival(4, s.b_tx, s.b_rx, c).wait_recv()
+
         lanes = chunk(c)
         grad_y = s.go[:, lanes] * s.filt[0, :, lanes]
-        grad_mixed = s.b_rx[c, 0:more, :].astype(F32) + s.skip[:, lanes] * grad_y
+        grad_mixed = s.b_rx[c].astype(F32) + s.skip[:, lanes] * grad_y
         finish(1, c, lanes, grad_mixed * s.filt[2, :, lanes])
         finish(2, c, lanes, grad_mixed * s.filt[1, :, lanes])
         return carry
 
+    heads = [send(s.head_tx.at[i], s.tail.at[i, TAIL : TAIL + PAD], s.edge_sent.at[3 + i],
+                  s.edge_came.at[3 + i], before_me) for i in range(3)]
     outs = [pltpu.make_async_copy(s.done.at[i], ref, s.out_sem.at[i])
             for i, ref in enumerate((s.dq_hbm, s.dk_hbm, s.dv_hbm))]
+
+    def mend(i):
+        heads[i].wait_recv()
+
+        @pl.when(me == count - 1)
+        def _():
+            s.tail[i, TAIL:, :] = jnp.zeros_like(s.tail[i, TAIL:, :])
+
+        total = None
+        for j in range(tap_count):
+            term = s.taps[i, j : j + 1, :] * s.tail[i, j : j + TAIL, :]
+            total = term if total is None else total + term
+        s.done[i, rows - TAIL :, :] = total.astype(BF16)
+        outs[i].start()
+
+    def long_send(some):
+        for peer in some:
+            exchange(5, s.l_tx, s.l_hbm, peer).start()
+
     arrive(3, s.y_tx, s.y_rx)
     lax.fori_loop(0, count, first_half, 0)
-    outs[0].start()
-    arrive(4, s.b_tx, s.b_rx)
+    heads[0].start()
     lax.fori_loop(0, count, second_half, 0)
-
     for peer in peers:
         exchange(6, s.part, s.one_rx, peer).start()
-    outs[1].start()
-    outs[2].start()
+    heads[1].start()
+    heads[2].start()
+    split = 4
+    long_send(peers[:split])
     s.one_rx[me] = s.part[me]
     arrive(6, s.part, s.one_rx)
     value = s.one_rx[0]
@@ -801,6 +812,9 @@
 
     for peer in peers:
         spread(peer).start()
+    long_send(peers[split:])
+    for i in range(3):
+        mend(i)
     sums_own = pltpu.make_async_copy(s.sum, s.sums_hbm.at[me], s.out_sem.at[4])
     sums_own.start()
 
@@ -809,18 +823,23 @@
     arrive(5, s.l_tx, s.l_hbm)
     for copy in outs + [l_own, sums_own]:
         copy.wait()
-    sends = ((s.h_tx, s.h_rx), (s.m_tx, s.m_rx), (s.g_tx, s.g_rx), (s.y_tx, s.y_rx),
-             (s.b_tx, s.b_rx), (s.l_tx, s.l_hbm), (s.part, s.one_rx))
-    for kind, (source, target) in enumerate(sends):
+    sends = ((0, s.h_tx, s.h_rx), (1, s.m_tx, s.m_rx), (3, s.y_tx, s.y_rx),
+             (4, s.b_tx, s.b_rx), (5, s.l_tx, s.l_hbm), (6, s.part, s.one_rx))
+    for kind, source, target in sends:
         for peer in peers:
             exchange(kind, source, target, peer).wait_send()
+    for h in range(rows // tall):
+        for peer in peers:
+            g_send(h, s.g_tx, s.g_rx, peer, me).wait_send()
     for peer in peers:
         spread(peer).wait_send()
-    for p in range(pieces):
+    for head in heads:
+        head.wait_send()
+    for h, p in batches:
         for slot, peer in enumerate(rest + [partner]):
-            own(slot, p, peer).wait_send()
+            own(slot, h, p, peer).wait_send()
         for slot, direct in enumerate(rest):
-            passed(slot, p, direct).wait_send()
+            passed(slot, h, p, direct).wait_send()
 
 
 def mix(spec, what):
@@ -874,22 +893,38 @@
     lax.fori_loop(0, half // step, chunk, 0)
 
 
-def result_kernel(dq_in, dk_in, dv_in, l_ref, sums_ref,
-                  dq_out, dk_out, dv_out, long_ref, short_ref, skip_ref, sem):
+def result_kernel(dq_in, dk_in, dv_in, l_in, sums_in,
+                  dq_out, dk_out, dv_out, long_out, short_ref, skip_ref,
+                  streams, l_ref, long_ref, sums_ref, in_sem, out_sem):
     count, rows, cw = l_ref.shape
     tap_count = short_ref.shape[1]
-    pairs = ((dq_in, dq_out), (dk_in, dk_out), (dv_in, dv_out))
-    copies = [pltpu.make_async_copy(a, b, sem.at[i]) for i, (a, b) in enumerate(pairs)]
-    for copy in copies:
-        copy.start()
+
+    def copy(a, b, sem):
+        return pltpu.make_async_copy(a, b, sem)
+
+    loads = [copy(l_in, l_ref, in_sem.at[3]), copy(sums_in, sums_ref, in_sem.at[4])]
+    loads += [copy(ref, streams.at[i], in_sem.at[i])
+              for i, ref in enumerate((dq_in, dk_in, dv_in))]
+    stores = [copy(streams.at[i], ref, out_sem.at[i])
+              for i, ref in enumerate((dq_out, dk_out, dv_out))]
+    long_store = copy(long_ref, long_out, out_sem.at[3])
+    for load in loads:
+        load.start()
+    loads[0].wait()
+    for c in range(count):
+        long_ref[:, c * cw : (c + 1) * cw] = l_ref[c].astype(F32)
+    long_store.start()
+    for load, store in zip(loads[2:], stores):
+        load.wait()
+        store.start()
+    loads[1].wait()
     for c in range(count):
         lanes = slice(c * cw, (c + 1) * cw)
-        long_ref[:, lanes] = l_ref[c].astype(F32)
         for i in range(3):
             short_ref[i, :, lanes] = sums_ref[c, i * tap_count : (i + 1) * tap_count, :]
         skip_ref[:, lanes] = sums_ref[c, 3 * tap_count : 3 * tap_count + 1, :]
-    for copy in copies:
-        copy.wait()
+    for store in stores + [long_store]:
+        store.wait()
 
 
 def joined(queries, keys, values, long_filter, short_filters, skip, w_out, d_out):
@@ -899,7 +934,7 @@
     cw = width // ctx
     tap_count = short_filters.shape[1]
     cols = d_out.shape[1]
-    pieces = 4
+    halves, pieces = 2, 4
     shape = jax.ShapeDtypeStruct
     dma = pltpu.SemaphoreType.DMA
     forward, inverse = (jnp.asarray(t) for t in tables(rows))
@@ -917,30 +952,30 @@
         ("l_hbm", shape((ctx, rows, cw), BF16)), ("sums_hbm", shape((ctx, 16, cw), F32)),
     ]
     bulk = pltpu.VMEM((ctx, rows, cw), BF16)
-    tailed = pltpu.VMEM((ctx, rows + TAIL, cw), BF16)
     small = pltpu.VMEM((ctx, 16, cw), F32)
     rim = pltpu.VMEM((3, TAIL, width), BF16)
     scratch = [
         ("long_own", pltpu.VMEM((rows, width), F32)), ("own", pltpu.VMEM((3, rows, width), BF16)),
         ("d_own", pltpu.VMEM((rows, cols), BF16)), ("fwd", pltpu.VMEM(forward.shape, BF16)),
-        ("inv", pltpu.VMEM(inverse.shape, BF16)), ("before", rim), ("after", rim),
-        ("ext", pltpu.VMEM((3, rows + 4 * PAD, width), F32)),
-        ("filt", pltpu.VMEM((3, rows + PAD, width), F32)),
-        ("held", pltpu.VMEM((parts, pieces, rows, cols // pieces), BF16)),
+        ("inv", pltpu.VMEM(inverse.shape, BF16)), ("before", rim), ("tail", pltpu.VMEM((3, TAIL + PAD, width), F32)),
+        ("head_tx", pltpu.VMEM((3, PAD, width), F32)),
+        ("ext", pltpu.VMEM((3, rows + PAD, width), F32)),
+        ("filt", pltpu.VMEM((3, rows, width), F32)),
+        ("held", pltpu.VMEM((parts, halves, pieces, rows // halves, cols // pieces), BF16)),
         ("weights", pltpu.VMEM((parts, width, cols), BF16)),
         ("total", pltpu.VMEM((rows, width), F32)),
-        ("go", pltpu.VMEM((rows + PAD, width), F32)),
-        ("go_head", pltpu.VMEM((TAIL, width), BF16)), ("go_after", pltpu.VMEM((TAIL, width), BF16)),
+        ("go", pltpu.VMEM((rows, width), F32)),
         ("h_tx", bulk), ("h_rx", bulk), ("m_tx", bulk), ("m_rx", bulk), ("g_tx", bulk),
-        ("g_rx", bulk), ("y_tx", tailed), ("y_rx", tailed), ("b_tx", tailed), ("b_rx", tailed),
+        ("g_rx", bulk), ("y_tx", bulk), ("y_rx", bulk), ("b_tx", bulk), ("b_rx", bulk),
         ("l_tx", bulk), ("spec", pltpu.VMEM((3, ctx, 2 * rows, cw), F32)),
-        ("grad", pltpu.VMEM((3, rows + 4 * PAD, cw), F32)),
+        ("grad", pltpu.VMEM((3, rows + PAD, cw), F32)),
         ("done", pltpu.VMEM((3, rows, width), BF16)),
         ("part", small), ("one_rx", small), ("sum", pltpu.VMEM((16, cw), F32)),
-        ("load_sem", dma((7,))), ("w_sem", dma((parts,))), ("edge_sent", dma((7,))),
-        ("edge_came", dma((7,))), ("own_sent", dma((parts // 2, pieces))),
-        ("pass_sent", dma((parts // 2, pieces))), ("d_came", dma((parts, pieces))),
+        ("load_sem", dma((7,))), ("w_sem", dma((parts,))), ("edge_sent", dma((6,))),
+        ("edge_came", dma((6,))), ("own_sent", dma((parts // 2, halves, pieces))),
+        ("pass_sent", dma((parts // 2, halves, pieces))), ("d_came", dma((parts, halves, pieces))),
         ("sent", dma((8, ctx))), ("came", dma((8, ctx))), ("out_sem", dma((5,))),
+        ("g_sent", dma((halves, ctx))), ("g_came", dma((halves, ctx))),
     ]
     names = tuple(name for name, *_ in inputs + outputs + scratch)
     dq, dk, dv, back, sums = pl.pallas_call(
@@ -955,9 +990,10 @@
         result_kernel,
         out_shape=[stream, stream, stream, shape((rows, width), F32),
                    shape((3, tap_count, width), F32), shape((1, width), F32)],
-        in_specs=[anyw, anyw, anyw, vmem, vmem],
-        out_specs=[anyw, anyw, anyw, vmem, vmem, vmem],
-        scratch_shapes=[dma((3,))],
+        in_specs=[anyw] * 5,
+        out_specs=[anyw] * 4 + [vmem] * 2,
+        scratch_shapes=[pltpu.VMEM((3, rows, width), BF16), pltpu.VMEM((ctx, rows, cw), BF16),
+                        pltpu.VMEM((rows, width), F32), small, dma((5,)), dma((4,))],
         compiler_params=pltpu.CompilerParams(**PARAMS),
     )(dq, dk, dv, back, sums)
     return dq, dk, dv, d_long, d_short, d_skip[0]

time: 141 us -> 89.4 us (0.63)
  Pallas kernels: 141 us -> 88.5 us
    pallas_call x1, Pallas kernels: 50.8 us -> 3.35 us  [joined(): pl.pallas_call(result_kernel, out_shape=[stream, stream, stream, shape((r...]
    pallas_call x1, Pallas kernels: 89.8 us -> 85.2 us  [joined(): pl.pallas_call(functools.partial(whole_kernel, names), out_shape=[out for...]
where the time goes in v2:
time: 89.4 us; the launch traced here: 89.2 us
  Pallas kernels  88.5 us (99%)
    pallas_call x1, Pallas kernels, joined(): pl.pallas_call(functools.partial(whole_kernel, names), out_shape=[out for...  85.2 us
    pallas_call x1, Pallas kernels, joined(): pl.pallas_call(result_kernel, out_shape=[stream, stream, stream, shape((r...  3.35 us

profile of v2, /device:TPU:0, one launch (start us, length us, event | category | flops | bytes accessed | tf_op | source)
XLA Modules:
  0.0 89.2 jit_solution(3567635168859947316)
XLA Ops:
  0.6 85.2 %shard_map.145 = (bf16[256,1024]{1,0:T(8,128)(2,1)}, bf16[256,1024]{1,0:T(8,128)(2,1)}, bf16[256,1024]{1,0:T(8,128)(2,1)}, bf16[8,256,128]{2,1,0:T(8,128)(2,1)}, f32[8,16,128]{2,1,0:T(8,128)}) custom-call(bf16[256,1024]{1,0:T(8,128)(2,1)} %refs_0_.1, bf16[256,1024]{1,0:T(8,128)(2,1)} %refs_1_.1, bf16[256,1024]{1,0:T(8,128)(2,1)} %refs_2_.1, ...), custom_call_target="tpu_custom_call" | custom-call | tf_op jit(solution)/shard_map/pallas_call | solution.py:981
  85.8 3.4 %shard_map.146 = (bf16[256,1024]{1,0:T(8,128)(2,1)}, bf16[256,1024]{1,0:T(8,128)(2,1)}, bf16[256,1024]{1,0:T(8,128)(2,1)}, f32[256,1024]{1,0:T(8,128)}, f32[3,3,1024]{2,1,0:T(4,128)}, /*index=5*/f32[1,1024]{1,0:T(1,128)}) custom-call(bf16[256,1024]{1,0:T(8,128)(2,1)} %get-tuple-element.17.dq_in, bf16[256,1024]{1,0:T(8,128)(2,1)} %get-tuple-element.18.dk_in, ...), custom_call_target="tpu_custom_call" | custom-call | tf_op jit(solution)/shard_map/pallas_call | solution.py:989

commit v3 on v2

--- a/solution.py
+++ b/solution.py
@@ -515,6 +515,7 @@
     after_me = lax.rem(me + 1, count)
     before_me = lax.rem(me + count - 1, count)
     peers = [lax.rem(me + o, count) for o in far_first(count)]
+    sources = [lax.rem(me + count - o, count) for o in far_first(count)]
     streams = (s.q_hbm, s.k_hbm, s.v_hbm)
 
     def load(source, target, i):
@@ -529,9 +530,12 @@
         lanes = pl.ds(pl.multiple_of(part * cols, cols), cols)
         return pltpu.make_async_copy(s.w_hbm.at[:, lanes], s.weights.at[part], s.w_sem.at[part])
 
+    small_loads = [load(s.taps_hbm, s.taps, 7), load(s.skip_hbm, s.skip, 8)]
     long_load.start()
     for i in (1, 2, 0):
         stream_loads[i].start()
+    for small in small_loads:
+        small.start()
     d_load.start()
     weight(mine).start()
     weight(partner).start()
@@ -615,6 +619,8 @@
     def _():
         s.before[...] = jnp.zeros_like(s.before)
 
+    for small in small_loads:
+        small.wait()
     for i in (1, 2, 0):
         fill_rim(i)
     for peer in peers + [me]:
@@ -711,10 +717,9 @@
     deliver(keep, s.y_tx, 2)
     s.y_rx[me] = s.y_tx[me]
 
-    for h in range(rows // tall):
-        for peer in peers:
+    for peer in sources:
+        for h in range(rows // tall):
             g_send(h, s.g_tx, s.g_rx, peer, peer).wait_recv()
-    for peer in peers:
         exchange(3, s.y_tx, s.y_rx, peer).start()
     spectra(s.fwd, [(s.g_rx.at[i], 2, i) for i in range(count)], s.spec)
     mix(s.spec, "b")
@@ -760,6 +765,10 @@
         def _():
             arrival(4, s.b_tx, s.b_rx, c).wait_recv()
 
+        @pl.when((c != me) & (k < split))
+        def _():
+            exchange(5, s.l_tx, s.l_hbm, c).start()
+
         lanes = chunk(c)
         grad_y = s.go[:, lanes] * s.filt[0, :, lanes]
         grad_mixed = s.b_rx[c].astype(F32) + s.skip[:, lanes] * grad_y
@@ -786,6 +795,8 @@
         s.done[i, rows - TAIL :, :] = total.astype(BF16)
         outs[i].start()
 
+    split, later = 0, 3 * count // 8
+
     def long_send(some):
         for peer in some:
             exchange(5, s.l_tx, s.l_hbm, peer).start()
@@ -794,25 +805,25 @@
     lax.fori_loop(0, count, first_half, 0)
     heads[0].start()
     lax.fori_loop(0, count, second_half, 0)
-    for peer in peers:
-        exchange(6, s.part, s.one_rx, peer).start()
+    s.part_tx[...] = s.part[...].astype(BF16)
+    for peer in peers:
+        exchange(6, s.part_tx, s.one_rx, peer).start()
     heads[1].start()
     heads[2].start()
-    split = 4
-    long_send(peers[:split])
-    s.one_rx[me] = s.part[me]
-    arrive(6, s.part, s.one_rx)
-    value = s.one_rx[0]
+    long_send(sources[split:later])
+    s.one_rx[me] = s.part_tx[me]
+    arrive(6, s.part_tx, s.one_rx)
+    value = s.one_rx[0].astype(F32)
     for c in range(1, count):
-        value = value + s.one_rx[c]
-    s.sum[...] = value
+        value = value + s.one_rx[c].astype(F32)
+    s.sum[...] = value.astype(BF16)
 
     def spread(peer):
         return send(s.sum, s.sums_hbm.at[me], s.sent.at[7, peer], s.came.at[7, me], peer)
 
     for peer in peers:
         spread(peer).start()
-    long_send(peers[split:])
+    long_send(sources[later:])
     for i in range(3):
         mend(i)
     sums_own = pltpu.make_async_copy(s.sum, s.sums_hbm.at[me], s.out_sem.at[4])
@@ -824,7 +835,7 @@
     for copy in outs + [l_own, sums_own]:
         copy.wait()
     sends = ((0, s.h_tx, s.h_rx), (1, s.m_tx, s.m_rx), (3, s.y_tx, s.y_rx),
-             (4, s.b_tx, s.b_rx), (5, s.l_tx, s.l_hbm), (6, s.part, s.one_rx))
+             (4, s.b_tx, s.b_rx), (5, s.l_tx, s.l_hbm), (6, s.part_tx, s.one_rx))
     for kind, source, target in sends:
         for peer in peers:
             exchange(kind, source, target, peer).wait_send()
@@ -894,36 +905,46 @@
 
 
 def result_kernel(dq_in, dk_in, dv_in, l_in, sums_in,
-                  dq_out, dk_out, dv_out, long_out, short_ref, skip_ref,
-                  streams, l_ref, long_ref, sums_ref, in_sem, out_sem):
+                  dq_out, dk_out, dv_out, long_out, short_out, skip_out,
+                  streams, l_ref, long_ref, sums_ref, short_ref, skip_ref,
+                  in_sem, out_sem, l_sem, long_sem):
     count, rows, cw = l_ref.shape
     tap_count = short_ref.shape[1]
-
-    def copy(a, b, sem):
-        return pltpu.make_async_copy(a, b, sem)
-
-    loads = [copy(l_in, l_ref, in_sem.at[3]), copy(sums_in, sums_ref, in_sem.at[4])]
-    loads += [copy(ref, streams.at[i], in_sem.at[i])
-              for i, ref in enumerate((dq_in, dk_in, dv_in))]
+    steps = l_sem.shape[0]
+    tall = rows // steps
+    copy = pltpu.make_async_copy
+    l_loads, l_stores = [], []
+    for n in range(steps):
+        at = slice(n * tall, (n + 1) * tall)
+        l_loads.append(copy(l_in.at[:, at], l_ref.at[:, at], l_sem.at[n]))
+        l_stores.append(copy(long_ref.at[at], long_out.at[at], long_sem.at[n]))
+    sums_load = copy(sums_in, sums_ref, in_sem.at[3])
+    loads = [copy(ref, streams.at[i], in_sem.at[i])
+             for i, ref in enumerate((dq_in, dk_in, dv_in))]
     stores = [copy(streams.at[i], ref, out_sem.at[i])
               for i, ref in enumerate((dq_out, dk_out, dv_out))]
-    long_store = copy(long_ref, long_out, out_sem.at[3])
-    for load in loads:
+    stores += [copy(short_ref, short_out, out_sem.at[3]), copy(skip_ref, skip_out, out_sem.at[4])]
+    for load in [sums_load] + l_loads + loads:
         load.start()
-    loads[0].wait()
+    sums_load.wait()
     for c in range(count):
-        long_ref[:, c * cw : (c + 1) * cw] = l_ref[c].astype(F32)
-    long_store.start()
-    for load, store in zip(loads[2:], stores):
+        lanes = slice(c * cw, (c + 1) * cw)
+        sums = sums_ref[c].astype(F32)
+        for i in range(3):
+            short_ref[i, :, lanes] = sums[i * tap_count : (i + 1) * tap_count, :]
+        skip_ref[:, lanes] = sums[3 * tap_count : 3 * tap_count + 1, :]
+    stores[3].start()
+    stores[4].start()
+    for n in range(steps):
+        l_loads[n].wait()
+        at = slice(n * tall, (n + 1) * tall)
+        for c in range(count):
+            long_ref[at, c * cw : (c + 1) * cw] = l_ref[c, at, :].astype(F32)
+        l_stores[n].start()
+    for load, store in zip(loads, stores):
         load.wait()
         store.start()
-    loads[1].wait()
-    for c in range(count):
-        lanes = slice(c * cw, (c + 1) * cw)
-        for i in range(3):
-            short_ref[i, :, lanes] = sums_ref[c, i * tap_count : (i + 1) * tap_count, :]
-        skip_ref[:, lanes] = sums_ref[c, 3 * tap_count : 3 * tap_count + 1, :]
-    for store in stores + [long_store]:
+    for store in stores + l_stores:
         store.wait()
 
 
@@ -939,22 +960,22 @@
     dma = pltpu.SemaphoreType.DMA
     forward, inverse = (jnp.asarray(t) for t in tables(rows))
     anyw = pl.BlockSpec(memory_space=pl.ANY)
-    vmem = pl.BlockSpec(memory_space=pltpu.VMEM)
     inputs = [
         ("q_hbm", queries, anyw), ("k_hbm", keys, anyw), ("v_hbm", values, anyw),
-        ("long_hbm", long_filter, anyw), ("taps", short_filters, vmem),
-        ("skip", skip[None], vmem), ("d_hbm", d_out, anyw), ("w_hbm", w_out, anyw),
+        ("long_hbm", long_filter, anyw), ("taps_hbm", short_filters, anyw),
+        ("skip_hbm", skip[None], anyw), ("d_hbm", d_out, anyw), ("w_hbm", w_out, anyw),
         ("fwd_hbm", forward, anyw), ("inv_hbm", inverse, anyw),
     ]
     stream = shape((rows, width), BF16)
     outputs = [
         ("dq_hbm", stream), ("dk_hbm", stream), ("dv_hbm", stream),
-        ("l_hbm", shape((ctx, rows, cw), BF16)), ("sums_hbm", shape((ctx, 16, cw), F32)),
+        ("l_hbm", shape((ctx, rows, cw), BF16)), ("sums_hbm", shape((ctx, 16, cw), BF16)),
     ]
     bulk = pltpu.VMEM((ctx, rows, cw), BF16)
-    small = pltpu.VMEM((ctx, 16, cw), F32)
+    small = pltpu.VMEM((ctx, 16, cw), BF16)
     rim = pltpu.VMEM((3, TAIL, width), BF16)
     scratch = [
+        ("taps", pltpu.VMEM(short_filters.shape, F32)), ("skip", pltpu.VMEM((1, width), F32)),
         ("long_own", pltpu.VMEM((rows, width), F32)), ("own", pltpu.VMEM((3, rows, width), BF16)),
         ("d_own", pltpu.VMEM((rows, cols), BF16)), ("fwd", pltpu.VMEM(forward.shape, BF16)),
         ("inv", pltpu.VMEM(inverse.shape, BF16)), ("before", rim), ("tail", pltpu.VMEM((3, TAIL + PAD, width), F32)),
@@ -970,8 +991,9 @@
         ("l_tx", bulk), ("spec", pltpu.VMEM((3, ctx, 2 * rows, cw), F32)),
         ("grad", pltpu.VMEM((3, rows + PAD, cw), F32)),
         ("done", pltpu.VMEM((3, rows, width), BF16)),
-        ("part", small), ("one_rx", small), ("sum", pltpu.VMEM((16, cw), F32)),
-        ("load_sem", dma((7,))), ("w_sem", dma((parts,))), ("edge_sent", dma((6,))),
+        ("part", pltpu.VMEM((ctx, 16, cw), F32)), ("part_tx", small), ("one_rx", small),
+        ("sum", pltpu.VMEM((16, cw), BF16)),
+        ("load_sem", dma((9,))), ("w_sem", dma((parts,))), ("edge_sent", dma((6,))),
         ("edge_came", dma((6,))), ("own_sent", dma((parts // 2, halves, pieces))),
         ("pass_sent", dma((parts // 2, halves, pieces))), ("d_came", dma((parts, halves, pieces))),
         ("sent", dma((8, ctx))), ("came", dma((8, ctx))), ("out_sem", dma((5,))),
@@ -991,9 +1013,11 @@
         out_shape=[stream, stream, stream, shape((rows, width), F32),
                    shape((3, tap_count, width), F32), shape((1, width), F32)],
         in_specs=[anyw] * 5,
-        out_specs=[anyw] * 4 + [vmem] * 2,
+        out_specs=[anyw] * 6,
         scratch_shapes=[pltpu.VMEM((3, rows, width), BF16), pltpu.VMEM((ctx, rows, cw), BF16),
-                        pltpu.VMEM((rows, width), F32), small, dma((5,)), dma((4,))],
+                        pltpu.VMEM((rows, width), F32), small,
+                        pltpu.VMEM((3, tap_count, width), F32), pltpu.VMEM((1, width), F32),
+                        dma((4,)), dma((5,)), dma((4,)), dma((4,))],
         compiler_params=pltpu.CompilerParams(**PARAMS),
     )(dq, dk, dv, back, sums)
     return dq, dk, dv, d_long, d_short, d_skip[0]

time: 89.4 us -> 85.7 us (0.959)
  Pallas kernels: 88.5 us -> 84.9 us
    pallas_call x1, Pallas kernels: 85.2 us -> 82.1 us  [joined(): pl.pallas_call(functools.partial(whole_kernel, names), out_shape=[out for...]
where the time goes in v3:
time: 85.7 us; the launch traced here: 85.5 us
  Pallas kernels  84.9 us (99%)
    pallas_call x1, Pallas kernels, joined(): pl.pallas_call(functools.partial(whole_kernel, names), out_shape=[out for...  82.1 us
    pallas_call x1, Pallas kernels, joined(): pl.pallas_call(result_kernel, out_shape=[stream, stream, stream, shape((r...  2.81 us

profile of v3, /device:TPU:0, one launch (start us, length us, event | category | flops | bytes accessed | tf_op | source)
XLA Modules:
  0.0 85.5 jit_solution(9615252524243278626)
XLA Ops:
  0.6 82.1 %shard_map.145 = (bf16[256,1024]{1,0:T(8,128)(2,1)}, bf16[256,1024]{1,0:T(8,128)(2,1)}, bf16[256,1024]{1,0:T(8,128)(2,1)}, bf16[8,256,128]{2,1,0:T(8,128)(2,1)}, bf16[8,16,128]{2,1,0:T(8,128)(2,1)}) custom-call(bf16[256,1024]{1,0:T(8,128)(2,1)} %refs_0_.1, bf16[256,1024]{1,0:T(8,128)(2,1)} %refs_1_.1, bf16[256,1024]{1,0:T(8,128)(2,1)} %refs_2_.1, ...), custom_call_target="tpu_custom_call" | custom-call | tf_op jit(solution)/shard_map/pallas_call | solution.py:1003
  82.7 2.8 %shard_map.146 = (bf16[256,1024]{1,0:T(8,128)(2,1)}, bf16[256,1024]{1,0:T(8,128)(2,1)}, bf16[256,1024]{1,0:T(8,128)(2,1)}, f32[256,1024]{1,0:T(8,128)}, f32[3,3,1024]{2,1,0:T(4,128)}, /*index=5*/f32[1,1024]{1,0:T(1,128)}) custom-call(bf16[256,1024]{1,0:T(8,128)(2,1)} %get-tuple-element.17.dq_in, bf16[256,1024]{1,0:T(8,128)(2,1)} %get-tuple-element.18.dk_in, ...), custom_call_target="tpu_custom_call" | custom-call | tf_op jit(solution)/shard_map/pallas_call | solution.py:1011

commit v4 on v3

--- a/solution.py
+++ b/solution.py
@@ -730,19 +730,23 @@
     l_own = pltpu.make_async_copy(s.l_tx.at[me], s.l_hbm.at[me], s.out_sem.at[3])
     l_own.start()
 
-    def finish(i, c, lanes, grad):
-        s.grad[i, 0:rows, :] = grad
-        s.grad[i, rows:, :] = jnp.zeros((PAD, cw), F32)
-        s.head_tx[i, :, lanes] = grad[0:PAD]
-        s.tail[i, 0:TAIL, lanes] = grad[rows - TAIL :]
-        total = None
+    def gather_sums(i, c, lanes, grad):
+        s.grads[i, 0:rows, lanes] = grad
+        s.head_tx[i * rim : (i + 1) * rim, lanes] = grad[0:rim]
         for j in range(tap_count):
-            term = s.taps[i, j : j + 1, lanes] * s.grad[i, j : j + rows, :]
-            total = term if total is None else total + term
             stream = s.ext[i, PAD - j : PAD - j + rows, lanes]
             row = i * tap_count + j
             s.part[c, row : row + 1, :] = jnp.sum(grad * stream, axis=0, keepdims=True)
-        s.done[i, :, lanes] = total.astype(BF16)
+
+    def write_out(c, carry):
+        lanes = chunk(c)
+        for i in range(3):
+            total = None
+            for j in range(tap_count):
+                term = s.taps[i, j : j + 1, lanes] * s.grads[i, j : j + rows, lanes]
+                total = term if total is None else total + term
+            s.done[i, :, lanes] = total.astype(BF16)
+        return carry
 
     def first_half(c, carry):
         lanes = chunk(c)
@@ -754,7 +758,7 @@
             grad_o * s.filt[0, :, lanes] * mixed, axis=0, keepdims=True
         )
         y_full = s.y_rx[c].astype(F32) + s.skip[:, lanes] * mixed
-        finish(0, c, lanes, grad_o * y_full)
+        gather_sums(0, c, lanes, grad_o * y_full)
         return carry
 
     def second_half(k, carry):
@@ -765,52 +769,42 @@
         def _():
             arrival(4, s.b_tx, s.b_rx, c).wait_recv()
 
-        @pl.when((c != me) & (k < split))
-        def _():
-            exchange(5, s.l_tx, s.l_hbm, c).start()
-
         lanes = chunk(c)
         grad_y = s.go[:, lanes] * s.filt[0, :, lanes]
         grad_mixed = s.b_rx[c].astype(F32) + s.skip[:, lanes] * grad_y
-        finish(1, c, lanes, grad_mixed * s.filt[2, :, lanes])
-        finish(2, c, lanes, grad_mixed * s.filt[1, :, lanes])
+        gather_sums(1, c, lanes, grad_mixed * s.filt[2, :, lanes])
+        gather_sums(2, c, lanes, grad_mixed * s.filt[1, :, lanes])
         return carry
 
-    heads = [send(s.head_tx.at[i], s.tail.at[i, TAIL : TAIL + PAD], s.edge_sent.at[3 + i],
-                  s.edge_came.at[3 + i], before_me) for i in range(3)]
+    heads = send(s.head_tx, s.head_rx, s.edge_sent.at[3], s.edge_came.at[3], before_me)
     outs = [pltpu.make_async_copy(s.done.at[i], ref, s.out_sem.at[i])
             for i, ref in enumerate((s.dq_hbm, s.dk_hbm, s.dv_hbm))]
 
-    def mend(i):
-        heads[i].wait_recv()
-
-        @pl.when(me == count - 1)
-        def _():
-            s.tail[i, TAIL:, :] = jnp.zeros_like(s.tail[i, TAIL:, :])
-
-        total = None
-        for j in range(tap_count):
-            term = s.taps[i, j : j + 1, :] * s.tail[i, j : j + TAIL, :]
-            total = term if total is None else total + term
-        s.done[i, rows - TAIL :, :] = total.astype(BF16)
-        outs[i].start()
-
-    split, later = 0, 3 * count // 8
-
-    def long_send(some):
-        for peer in some:
-            exchange(5, s.l_tx, s.l_hbm, peer).start()
+    even = lax.rem(mine, 2) == 0
+    steps_even, steps_odd = (0, 3, 3, 5, count), (0, 0, 0, 1, count)
+
+    def long_send(stage):
+        for n, peer in enumerate(sources):
+            due_even = steps_even[stage] <= n < steps_even[stage + 1]
+            due_odd = steps_odd[stage] <= n < steps_odd[stage + 1]
+            if not due_even and not due_odd:
+                continue
+
+            @pl.when((even & due_even) | (jnp.logical_not(even) & due_odd))
+            def _():
+                exchange(5, s.l_tx, s.l_hbm, peer).start()
 
     arrive(3, s.y_tx, s.y_rx)
+    long_send(0)
+    s.head_tx[...] = jnp.zeros_like(s.head_tx)
     lax.fori_loop(0, count, first_half, 0)
-    heads[0].start()
     lax.fori_loop(0, count, second_half, 0)
+    long_send(1)
     s.part_tx[...] = s.part[...].astype(BF16)
     for peer in peers:
         exchange(6, s.part_tx, s.one_rx, peer).start()
-    heads[1].start()
-    heads[2].start()
-    long_send(sources[split:later])
+    heads.start()
+    long_send(2)
     s.one_rx[me] = s.part_tx[me]
     arrive(6, s.part_tx, s.one_rx)
     value = s.one_rx[0].astype(F32)
@@ -823,9 +817,18 @@
 
     for peer in peers:
         spread(peer).start()
-    long_send(sources[later:])
-    for i in range(3):
-        mend(i)
+    long_send(3)
+    heads.wait_recv()
+    s.grads[:, rows:, :] = jnp.zeros_like(s.grads[:, rows:, :])
+
+    @pl.when(me != count - 1)
+    def _():
+        for i in range(3):
+            s.grads[i, rows : rows + rim, :] = s.head_rx[i * rim : (i + 1) * rim, :]
+
+    lax.fori_loop(0, count, write_out, 0)
+    for copy in outs:
+        copy.start()
     sums_own = pltpu.make_async_copy(s.sum, s.sums_hbm.at[me], s.out_sem.at[4])
     sums_own.start()
 
@@ -844,8 +847,7 @@
             g_send(h, s.g_tx, s.g_rx, peer, me).wait_send()
     for peer in peers:
         spread(peer).wait_send()
-    for head in heads:
-        head.wait_send()
+    heads.wait_send()
     for h, p in batches:
         for slot, peer in enumerate(rest + [partner]):
             own(slot, h, p, peer).wait_send()
@@ -974,12 +976,13 @@
     bulk = pltpu.VMEM((ctx, rows, cw), BF16)
     small = pltpu.VMEM((ctx, 16, cw), BF16)
     rim = pltpu.VMEM((3, TAIL, width), BF16)
+    rim_rows = -(-3 * (tap_count - 1) // PAD) * PAD
     scratch = [
         ("taps", pltpu.VMEM(short_filters.shape, F32)), ("skip", pltpu.VMEM((1, width), F32)),
         ("long_own", pltpu.VMEM((rows, width), F32)), ("own", pltpu.VMEM((3, rows, width), BF16)),
         ("d_own", pltpu.VMEM((rows, cols), BF16)), ("fwd", pltpu.VMEM(forward.shape, BF16)),
-        ("inv", pltpu.VMEM(inverse.shape, BF16)), ("before", rim), ("tail", pltpu.VMEM((3, TAIL + PAD, width), F32)),
-        ("head_tx", pltpu.VMEM((3, PAD, width), F32)),
+        ("inv", pltpu.VMEM(inverse.shape, BF16)), ("before", rim), ("head_tx", pltpu.VMEM((rim_rows, width), F32)),
+        ("head_rx", pltpu.VMEM((rim_rows, width), F32)),
         ("ext", pltpu.VMEM((3, rows + PAD, width), F32)),
         ("filt", pltpu.VMEM((3, rows, width), F32)),
         ("held", pltpu.VMEM((parts, halves, pieces, rows // halves, cols // pieces), BF16)),
@@ -989,7 +992,7 @@
         ("h_tx", bulk), ("h_rx", bulk), ("m_tx", bulk), ("m_rx", bulk), ("g_tx", bulk),
         ("g_rx", bulk), ("y_tx", bulk), ("y_rx", bulk), ("b_tx", bulk), ("b_rx", bulk),
         ("l_tx", bulk), ("spec", pltpu.VMEM((3, ctx, 2 * rows, cw), F32)),
-        ("grad", pltpu.VMEM((3, rows + PAD, cw), F32)),
+        ("grads", pltpu.VMEM((3, rows + PAD, width), F32)),
         ("done", pltpu.VMEM((3, rows, width), BF16)),
         ("part", pltpu.VMEM((ctx, 16, cw), F32)), ("part_tx", small), ("one_rx", small),
         ("sum", pltpu.VMEM((16, cw), BF16)),
@@ -1027,7 +1030,7 @@
     ctx = lax.axis_size("ctx")
     rows, width = queries.shape
     cw = width // ctx
-    if cw % 128 == 0 and ctx <= 8:
+    if cw % 128 == 0 and ctx <= 8 and ctx % 2 == 0:
         return joined(queries, keys, values, long_filter, short_filters, skip, w_out, d_out)
     tap_count = short_filters.shape[1]
     parts = lax.axis_size("ch")

time: 85.7 us -> 84 us (0.980)
  Pallas kernels: 84.9 us -> 83.2 us
    pallas_call x1, Pallas kernels: 82.1 us -> 80.4 us  [joined(): pl.pallas_call(functools.partial(whole_kernel, names), out_shape=[out for...]
where the time goes in v4:
time: 84 us; the launch traced here: 83.9 us
  Pallas kernels  83.2 us (99%)
    pallas_call x1, Pallas kernels, joined(): pl.pallas_call(functools.partial(whole_kernel, names), out_shape=[out for...  80.4 us
    pallas_call x1, Pallas kernels, joined(): pl.pallas_call(result_kernel, out_shape=[stream, stream, stream, shape((r...  2.81 us

profile of v4, /device:TPU:0, one launch (start us, length us, event | category | flops | bytes accessed | tf_op | source)
XLA Modules:
  0.0 83.9 jit_solution(215013665345333222)
XLA Ops:
  0.6 80.4 %shard_map.145 = (bf16[256,1024]{1,0:T(8,128)(2,1)}, bf16[256,1024]{1,0:T(8,128)(2,1)}, bf16[256,1024]{1,0:T(8,128)(2,1)}, bf16[8,256,128]{2,1,0:T(8,128)(2,1)}, bf16[8,16,128]{2,1,0:T(8,128)(2,1)}) custom-call(bf16[256,1024]{1,0:T(8,128)(2,1)} %refs_0_.1, bf16[256,1024]{1,0:T(8,128)(2,1)} %refs_1_.1, bf16[256,1024]{1,0:T(8,128)(2,1)} %refs_2_.1, ...), custom_call_target="tpu_custom_call" | custom-call | tf_op jit(solution)/shard_map/pallas_call | solution.py:1006
  81.1 2.8 %shard_map.146 = (bf16[256,1024]{1,0:T(8,128)(2,1)}, bf16[256,1024]{1,0:T(8,128)(2,1)}, bf16[256,1024]{1,0:T(8,128)(2,1)}, f32[256,1024]{1,0:T(8,128)}, f32[3,3,1024]{2,1,0:T(4,128)}, /*index=5*/f32[1,1024]{1,0:T(1,128)}) custom-call(bf16[256,1024]{1,0:T(8,128)(2,1)} %get-tuple-element.17.dq_in, bf16[256,1024]{1,0:T(8,128)(2,1)} %get-tuple-element.18.dk_in, ...), custom_call_target="tpu_custom_call" | custom-call | tf_op jit(solution)/shard_map/pallas_call | solution.py:1014

commit v5 on v4

--- a/solution.py
+++ b/solution.py
@@ -763,6 +763,7 @@
 
     def second_half(k, carry):
         middle = count // 2
+        k = lax.rem(k + count - 1, count)
         c = lax.rem(me + count - middle + (2 * lax.rem(k, 2) - 1) * ((k + 1) // 2), count)
 
         @pl.when(c != me)

time: 84 us -> 84.1 us (level)
  no operation moved by 1% of the time
where the time goes in v5:
time: 84.1 us; the launch traced here: 84 us
  Pallas kernels  83.3 us (99%)
    pallas_call x1, Pallas kernels, joined(): pl.pallas_call(functools.partial(whole_kernel, names), out_shape=[out for...  80.5 us
    pallas_call x1, Pallas kernels, joined(): pl.pallas_call(result_kernel, out_shape=[stream, stream, stream, shape((r...  2.81 us

profile of v5, /device:TPU:0, one launch (start us, length us, event | category | flops | bytes accessed | tf_op | source)
XLA Modules:
  0.0 84.0 jit_solution(8359400312701907281)
XLA Ops:
  0.6 80.5 %shard_map.145 = (bf16[256,1024]{1,0:T(8,128)(2,1)}, bf16[256,1024]{1,0:T(8,128)(2,1)}, bf16[256,1024]{1,0:T(8,128)(2,1)}, bf16[8,256,128]{2,1,0:T(8,128)(2,1)}, bf16[8,16,128]{2,1,0:T(8,128)(2,1)}) custom-call(bf16[256,1024]{1,0:T(8,128)(2,1)} %refs_0_.1, bf16[256,1024]{1,0:T(8,128)(2,1)} %refs_1_.1, bf16[256,1024]{1,0:T(8,128)(2,1)} %refs_2_.1, ...), custom_call_target="tpu_custom_call" | custom-call | tf_op jit(solution)/shard_map/pallas_call | solution.py:1007
  81.1 2.8 %shard_map.146 = (bf16[256,1024]{1,0:T(8,128)(2,1)}, bf16[256,1024]{1,0:T(8,128)(2,1)}, bf16[256,1024]{1,0:T(8,128)(2,1)}, f32[256,1024]{1,0:T(8,128)}, f32[3,3,1024]{2,1,0:T(4,128)}, /*index=5*/f32[1,1024]{1,0:T(1,128)}) custom-call(bf16[256,1024]{1,0:T(8,128)(2,1)} %get-tuple-element.17.dq_in, bf16[256,1024]{1,0:T(8,128)(2,1)} %get-tuple-element.18.dk_in, ...), custom_call_target="tpu_custom_call" | custom-call | tf_op jit(solution)/shard_map/pallas_call | solution.py:1015
